TPU v7x, 128 devices: a whole 4x4x4 slice. The times are simulated.
128 devices in a mesh: field: 4 (over x), shard: 32 (over z, y, core).
Axes of the slice: x: 4, y: 4, z: 4, core: 2. Of those that a mesh axis runs over, the one named last changes fastest.
Arguments:
- focal_uv: float32 [2048, 6, 2, 128], P(('field', 'shard')), may hold values from -1 to 1
- offsets: float32 [2048, 6, 2, 128], P(('field', 'shard')), may hold values from -6 to 6
- w_diag: float32 [2048, 6, 2, 128], P(('field', 'shard')), may hold values from 0.5 to 8
- w_corr: float32 [2048, 6, 128], P(('field', 'shard')), may hold values from -0.6 to 0.6
- star_count: int32 [2048], P(('field', 'shard')), may hold values from 16 to 128
- exposure_ids: int32 [2048, 6], P(('field', 'shard')), may hold values from 0 to 16383, as said below
- ccd_ids: int32 [2048, 6], P(('field', 'shard')), may hold values from 0 to 188
- exp_slot: int32 [16384], replicated, may hold values from 0 to 16383, as said below
Outputs:
- star_update: float32 [2048, 2, 128], P(('field', 'shard'))
- exposure_update: float32 [56, 16384], P(None, ('field', 'shard'))
- ccd_update: float32 [189, 6], replicated
Inputs may be any that keep to these rules, and one draw needn't show every extreme that they name: `exposure_ids`: exposure e belongs to owner (exp_slot[e] // 128) % 32 and field block exp_slot[e] // 4096. Among the 96 tile visits of one device (aligned blocks of 16 tiles), at most 4 have exposures of one owner, and exactly 4 for half of the owners; at most 2 have exposures of one owner in one field block, and exactly 2 for some pairs. `exp_slot`: A permutation.
All inputs are finite; a program needn't handle non-finite values.
Results may differ from a plain program's by a relative error of at most 0.0003.
Values sent between devices are 32-bit elements; how exact they have to be, the bound alone decides.
No kernel may reach another device: no remote copies, remote signals or barrier semaphores. Data moves between devices by JAX's collectives and lax.ppermute only.
A program may use at most 256 MiB of HBM per device.

v0:
```python
import math

import jax
import jax.numpy as jnp
from jax import lax
from jax.sharding import PartitionSpec as P

ORDER = 6
POLY = 28
NCCD = 189
EXP_DEV = 128


STAR_DAMP = 0.1
EXPOSURE_DAMP = 1.0
DETECTOR_DAMP = 1.0
HIGH = lax.Precision.HIGHEST


def legendre_terms(coord_u, coord_v):

    def series(value):
        values = [jnp.ones_like(value), value]
        for degree in range(1, ORDER):
            values.append(
                ((2 * degree + 1) * value * values[degree] - degree * values[degree - 1])
                / (degree + 1)
            )
        return values

    series_u = series(coord_u)
    series_v = series(coord_v)
    terms = []
    for total in range(ORDER + 1):
        for first in range(total + 1):
            second = total - first
            terms.append(
                math.sqrt((2 * first + 1) * (2 * second + 1)) * series_u[first] * series_v[second]
            )
    return jnp.stack(terms, axis=-2)


def plane_terms(coord_u, coord_v):
    return jnp.stack([jnp.ones_like(coord_u), coord_u, coord_v], axis=-2)


def star_terms(offsets, w_diag, w_corr, star_count):
    stars = offsets.shape[-1]
    present = (jnp.arange(stars, dtype=jnp.int32)[None, :] < star_count[:, None]).astype(
        jnp.float32
    )[:, None, :]
    weight_xx = w_diag[:, :, 0] * present
    weight_yy = w_diag[:, :, 1] * present
    weight_xy = w_corr * jnp.sqrt(w_diag[:, :, 0] * w_diag[:, :, 1]) * present
    resid_x = offsets[:, :, 0]
    resid_y = offsets[:, :, 1]
    hess_xx = jnp.sum(weight_xx, 1) + STAR_DAMP
    hess_yy = jnp.sum(weight_yy, 1) + STAR_DAMP
    hess_xy = jnp.sum(weight_xy, 1)
    determ = hess_xx * hess_yy - hess_xy * hess_xy
    inv_xx = (hess_yy / determ)[:, None]
    inv_yy = (hess_xx / determ)[:, None]
    inv_xy = (-hess_xy / determ)[:, None]
    grad_x = jnp.sum(weight_xx * resid_x + weight_xy * resid_y, 1)[:, None]
    grad_y = jnp.sum(weight_xy * resid_x + weight_yy * resid_y, 1)[:, None]
    left_x = resid_x - (inv_xx * grad_x + inv_xy * grad_y)
    left_y = resid_y - (inv_xy * grad_x + inv_yy * grad_y)
    pull_x = weight_xx * left_x + weight_xy * left_y
    pull_y = weight_xy * left_x + weight_yy * left_y
    prod_11 = inv_xx * weight_xx + inv_xy * weight_xy
    prod_12 = inv_xx * weight_xy + inv_xy * weight_yy
    prod_21 = inv_xy * weight_xx + inv_yy * weight_xy
    prod_22 = inv_xy * weight_xy + inv_yy * weight_yy
    schur_xx = weight_xx - (weight_xx * prod_11 + weight_xy * prod_21)
    schur_yy = weight_yy - (weight_xy * prod_12 + weight_yy * prod_22)
    schur_xy = weight_xy - (weight_xx * prod_12 + weight_xy * prod_22)
    return (
        (inv_xx, inv_yy, inv_xy),
        (weight_xx, weight_yy, weight_xy),
        (schur_xx, schur_yy, schur_xy, pull_x, pull_y),
    )


def normal_vectors(basis, schur_xx, schur_yy, schur_xy, pull_x, pull_y):

    def outer(scale):
        product = jnp.einsum(
            "...ps,...qs->...pq", basis * scale[..., None, :], basis, precision=HIGH
        )
        return product.reshape(scale.shape[:-1] + (-1,))

    grad_x = jnp.einsum("...ps,...s->...p", basis, pull_x, precision=HIGH)
    grad_y = jnp.einsum("...ps,...s->...p", basis, pull_y, precision=HIGH)
    return jnp.concatenate(
        [outer(schur_xx), outer(schur_yy), outer(schur_xy), grad_x, grad_y], axis=-1
    )


def batched_cholesky_solve(matrix, rhs):
    order_n = matrix.shape[0]
    rows_idx = jnp.arange(order_n, dtype=jnp.int32)
    work = matrix
    columns = []
    for step in range(order_n):
        pivot = jnp.sqrt(work[step, step])
        column = work[:, step] / pivot[None, :]
        column = jnp.where((rows_idx >= step)[:, None], column, jnp.float32(0.0))
        columns.append(column)
        work = work - column[:, None, :] * column[None, :, :]
    lower = jnp.stack(columns, axis=1)
    remain = rhs
    forward = []
    for step in range(order_n):
        value = remain[step] / lower[step, step]
        forward.append(value)
        remain = remain - lower[:, step] * value[None, :]
    remain = jnp.stack(forward, axis=0)
    backward = [None] * order_n
    for step in range(order_n - 1, -1, -1):
        value = remain[step] / lower[step, step]
        backward[step] = value
        remain = remain - lower[step] * value[None, :]
    return jnp.stack(backward, axis=0)


def solve_blocks(vectors, width, damping):
    square = width * width
    flipped = vectors.T
    count = vectors.shape[0]
    part_xx = flipped[:square].reshape(width, width, count)
    part_yy = flipped[square : 2 * square].reshape(width, width, count)
    part_xy = flipped[2 * square : 3 * square].reshape(width, width, count)
    matrix = jnp.concatenate(
        [jnp.concatenate([part_xx, part_xy], 1), jnp.concatenate([part_xy, part_yy], 1)], 0
    )
    matrix = matrix + damping * jnp.eye(2 * width, dtype=jnp.float32)[:, :, None]
    rhs = flipped[3 * square : 3 * square + 2 * width]
    return batched_cholesky_solve(matrix, rhs).T


def star_solve(inverse, weights, offsets, model_x, model_y):
    inv_xx, inv_yy, inv_xy = inverse
    weight_xx, weight_yy, weight_xy = weights
    left_x = offsets[:, :, 0] - model_x
    left_y = offsets[:, :, 1] - model_y
    grad_x = jnp.sum(weight_xx * left_x + weight_xy * left_y, 1)
    grad_y = jnp.sum(weight_xy * left_x + weight_yy * left_y, 1)
    return jnp.stack(
        [
            inv_xx[:, 0] * grad_x + inv_xy[:, 0] * grad_y,
            inv_xy[:, 0] * grad_x + inv_yy[:, 0] * grad_y,
        ],
        axis=1,
    )


def shards(focal_uv, offsets, w_diag, w_corr, star_count, exposure_ids, ccd_ids, exp_slot):
    shard_count = lax.axis_size("shard")
    field_count = lax.axis_size("field")
    tiles = offsets.shape[0]
    visits = offsets.shape[1]
    visits_all = tiles * visits
    capacity = 4 * visits_all // (3 * shard_count)
    slot_total = shard_count * capacity
    exp_local = EXP_DEV
    sentinel = field_count * exp_local
    vec_width = 3 * POLY * POLY + 2 * POLY
    padded_width = (vec_width + 128) // 128 * 128
    terms = star_terms(offsets, w_diag, w_corr, star_count)
    reduced = terms[2]
    coord_u = focal_uv[:, :, 0]
    coord_v = focal_uv[:, :, 1]
    basis = legendre_terms(coord_u, coord_v)
    plane = plane_terms(coord_u, coord_v)
    ccd_vec = normal_vectors(plane, *reduced).reshape(visits_all, -1)
    ccd_local = jax.ops.segment_sum(ccd_vec, ccd_ids.reshape(-1), num_segments=NCCD)
    ccd_table = lax.psum(ccd_local, ("field", "shard"))
    ccd_update = solve_blocks(ccd_table, 3, DETECTOR_DAMP)
    position = exp_slot[exposure_ids.reshape(-1)]
    owner = position // exp_local % shard_count
    row_index = position // (exp_local * shard_count) * exp_local + position % exp_local
    one_hot = (owner[:, None] == jnp.arange(shard_count, dtype=jnp.int32)[None, :]).astype(
        jnp.int32
    )
    earlier = jnp.cumsum(one_hot, axis=0) - one_hot
    target = owner * capacity + jnp.sum(earlier * one_hot, axis=1)
    local = normal_vectors(basis, *reduced).reshape(visits_all, vec_width)
    payload = jnp.concatenate(
        [
            local,
            row_index.astype(jnp.float32)[:, None],
            jnp.zeros((visits_all, padded_width - vec_width - 1), jnp.float32),
        ],
        axis=1,
    )
    outgoing = (
        jnp.zeros((slot_total, padded_width), jnp.float32)
        .at[:, vec_width]
        .set(float(sentinel))
        .at[target]
        .set(payload)
    )
    carried = lax.all_to_all(outgoing, "shard", split_axis=0, concat_axis=0, tiled=True)
    arrived_rows = carried[:, vec_width].astype(jnp.int32)
    table = jax.ops.segment_sum(carried, arrived_rows, num_segments=sentinel + 1)[:sentinel]
    summed = lax.psum_scatter(table, "field", scatter_dimension=0, tiled=True)
    solution = solve_blocks(summed[:, :vec_width], POLY, EXPOSURE_DAMP)
    exposure_update = solution.T
    everything = lax.all_gather(exposure_update, ("field", "shard"), axis=1, tiled=True)
    coeff = everything[:, position].T
    coeff = coeff.reshape(tiles, visits, 2 * POLY)
    det_coeff = ccd_update[ccd_ids]
    model_x = jnp.einsum("tkp,tkps->tks", coeff[..., :POLY], basis, precision=HIGH) + jnp.einsum(
        "tkp,tkps->tks", det_coeff[..., :3], plane, precision=HIGH
    )
    model_y = jnp.einsum("tkp,tkps->tks", coeff[..., POLY:], basis, precision=HIGH) + jnp.einsum(
        "tkp,tkps->tks", det_coeff[..., 3:], plane, precision=HIGH
    )
    star_update = star_solve(terms[0], terms[1], offsets, model_x, model_y)
    return (star_update, exposure_update, ccd_update)


def solution(mesh):
    in_specs = (
        P(("field", "shard"), None, None, None),
        P(("field", "shard"), None, None, None),
        P(("field", "shard"), None, None, None),
        P(("field", "shard"), None, None),
        P(("field", "shard")),
        P(("field", "shard"), None),
        P(("field", "shard"), None),
        P(),
    )
    out_specs = (P(("field", "shard"), None, None), P(None, ("field", "shard")), P())
    return jax.shard_map(shards, mesh=mesh, in_specs=in_specs, out_specs=out_specs, check_vma=False)
```

profile of v0, /device:TPU:1, one launch (start us, length us, event | category | flops | bytes accessed | tf_op | source)
XLA Modules:
  0.0 791.2 jit_solution(11336156431585171111)
XLA Ops:
  19.4 2.9 fusion.12
  22.4 2.9 fusion.10
  26.8 4.6 fusion.2
  31.5 2.4 concatenate.52
  33.8 6.1 fusion.4
  39.9 3.1 concatenate.51
  43.0 4.6 fusion.14
  47.6 2.4 concatenate.50
  51.4 2.3 scatter_fusion
  55.1 9.7 %all-to-all-start = ((f32[32,4,2432]{2,1,0:T(4,128)}), f32[32,4,2432]{2,1,0:T(4,128)S(1)}, u32[]{:S(2)}, u32[]{:S(2)}) async-start(f32[32,4,2432]{2,1,0:T(4,128)} %all_to_all.8), calls=%async_computation | async-start | bytes 2490368 | tf_op jit(solution)/shard_map/all_to_all | solution.py:203
  72.6 67.1 %psum.7 = f32[33,189]{1,0:T(8,128)S(1)} all-reduce(f32[33,189]{1,0:T(8,128)S(1)} %bitcast.1305), channel_id=1, replica_groups=mesh['field'=4,'shard'=32] {'field','shard'}, use_global_device_ids=true, to_apply=%region_12.13 | all-reduce | flops 6237 | bytes 49896 | tf_op jit(solution)/shard_map/psum | solution.py:177
  143.7 5.7 scatter_custom_fusion.1
  149.4 5.0 slice.1708
  154.5 5.9 copy.1072
  180.9 29.3 %reduce-scatter.2.cloned.1.call-done = f32[128,2432]{0,1:T(8,128)} async-done(((f32[512,2432]{0,1:T(8,128)}), f32[128,2432]{0,1:T(8,128)}) %reduce-scatter.2.cloned.1.call-update) | async-done | bytes 1245200 | tf_op jit(solution)/shard_map/reduce_scatter | solution.py:206
  252.0 1.9 multiply_subtract_fusion.40
  255.1 2.0 multiply_subtract_fusion.39
  259.0 2.3 multiply_subtract_fusion.38
  262.5 2.2 multiply_subtract_fusion.37
  265.6 2.4 multiply_subtract_fusion.36
  268.9 2.5 multiply_subtract_fusion.35
  272.3 2.7 multiply_subtract_fusion.34
  275.8 3.2 multiply_subtract_fusion.33
  279.9 2.9 multiply_subtract_fusion.32
  284.7 3.1 multiply_subtract_fusion.31
  289.7 3.4 multiply_subtract_fusion.30
  294.9 3.7 multiply_subtract_fusion.29
  300.5 3.7 multiply_subtract_fusion.28
  306.1 3.9 multiply_subtract_fusion.27
  311.9 4.3 multiply_subtract_fusion.26
  318.2 4.3 multiply_subtract_fusion.25
  324.3 4.8 multiply_subtract_fusion.24
  331.0 4.8 multiply_subtract_fusion.23
  337.6 5.0 multiply_subtract_fusion.22
  344.5 5.2 multiply_subtract_fusion.21
  351.5 5.4 multiply_subtract_fusion.20
  358.7 6.0 multiply_subtract_fusion.19
  366.6 10.4 %multiply_subtract_fusion.18 = f32[56,56,128]{2,0,1:T(8,128)S(1)} fusion(f32[56,128]{1,0:T(8,128)S(1)} %fusion.174, f32[56,128]{1,0:T(8,128)S(1)} %fusion.336, f32[56,128]{1,0:T(8,128)S(1)} %fusion.175, f32[56,128]{1,0:T(8,128)S(1)} %fusion.337, f32[56,128]{1,0:T(8,128)S(1)} %fusion.176, f32[56,128]{1,0:T(8,128)S(1)} %fusion.338, f32[56,128]{1,0:T(8,128)S(1)} %fusion.177, ...), kind=kLoop, calls=%fused_computation.28 | loop fusion | flops 30105600 | bytes 5345536 | tf_op jit(solution)/shard_map/sub | solution.py:109
  378.9 10.8 %multiply_subtract_fusion.17 = f32[56,56,128]{2,0,1:T(8,128)S(1)} fusion(f32[56,128]{1,0:T(8,128)S(1)} %fusion.173, f32[56,128]{1,0:T(8,128)S(1)} %fusion.335, f32[56,128]{1,0:T(8,128)S(1)} %fusion.174, f32[56,128]{1,0:T(8,128)S(1)} %fusion.336, f32[56,128]{1,0:T(8,128)S(1)} %fusion.175, f32[56,128]{1,0:T(8,128)S(1)} %fusion.337, f32[56,128]{1,0:T(8,128)S(1)} %fusion.176, ...), kind=kLoop, calls=%fused_computation.27 | loop fusion | flops 30908416 | bytes 5402880 | tf_op jit(solution)/shard_map/sub | solution.py:109
  391.6 11.0 %multiply_subtract_fusion.16 = f32[56,56,128]{2,0,1:T(8,128)S(1)} fusion(f32[56,128]{1,0:T(8,128)S(1)} %fusion.172, f32[56,128]{1,0:T(8,128)S(1)} %fusion.334, f32[56,128]{1,0:T(8,128)S(1)} %fusion.173, f32[56,128]{1,0:T(8,128)S(1)} %fusion.335, f32[56,128]{1,0:T(8,128)S(1)} %fusion.174, f32[56,128]{1,0:T(8,128)S(1)} %fusion.336, f32[56,128]{1,0:T(8,128)S(1)} %fusion.175, ...), kind=kLoop, calls=%fused_computation.26 | loop fusion | flops 31711232 | bytes 5460224 | tf_op jit(solution)/shard_map/sub | solution.py:109
  404.5 11.5 %multiply_subtract_fusion.15 = f32[56,56,128]{2,0,1:T(8,128)S(1)} fusion(f32[56,128]{1,0:T(8,128)S(1)} %fusion.171, f32[56,128]{1,0:T(8,128)S(1)} %fusion.333, f32[56,128]{1,0:T(8,128)S(1)} %fusion.172, f32[56,128]{1,0:T(8,128)S(1)} %fusion.334, f32[56,128]{1,0:T(8,128)S(1)} %fusion.173, f32[56,128]{1,0:T(8,128)S(1)} %fusion.335, f32[56,128]{1,0:T(8,128)S(1)} %fusion.174, ...), kind=kLoop, calls=%fused_computation.25 | loop fusion | flops 32514048 | bytes 5517568 | tf_op jit(solution)/shard_map/sub | solution.py:109
  417.9 11.7 %multiply_subtract_fusion.14 = f32[56,56,128]{2,0,1:T(8,128)S(1)} fusion(f32[56,128]{1,0:T(8,128)S(1)} %fusion.170, f32[56,128]{1,0:T(8,128)S(1)} %fusion.332, f32[56,128]{1,0:T(8,128)S(1)} %fusion.171, f32[56,128]{1,0:T(8,128)S(1)} %fusion.333, f32[56,128]{1,0:T(8,128)S(1)} %fusion.172, f32[56,128]{1,0:T(8,128)S(1)} %fusion.334, f32[56,128]{1,0:T(8,128)S(1)} %fusion.173, ...), kind=kLoop, calls=%fused_computation.24 | loop fusion | flops 33316864 | bytes 5574912 | tf_op jit(solution)/shard_map/sub | solution.py:109
  431.4 12.0 %multiply_subtract_fusion.13 = f32[56,56,128]{2,0,1:T(8,128)S(1)} fusion(f32[56,128]{1,0:T(8,128)S(1)} %fusion.169, f32[56,128]{1,0:T(8,128)S(1)} %fusion.331, f32[56,128]{1,0:T(8,128)S(1)} %fusion.170, f32[56,128]{1,0:T(8,128)S(1)} %fusion.332, f32[56,128]{1,0:T(8,128)S(1)} %fusion.171, f32[56,128]{1,0:T(8,128)S(1)} %fusion.333, f32[56,128]{1,0:T(8,128)S(1)} %fusion.172, ...), kind=kLoop, calls=%fused_computation.23 | loop fusion | flops 34119680 | bytes 5632256 | tf_op jit(solution)/shard_map/sub | solution.py:109
  445.3 12.2 %multiply_subtract_fusion.12 = f32[56,56,128]{2,0,1:T(8,128)S(1)} fusion(f32[56,128]{1,0:T(8,128)S(1)} %fusion.168, f32[56,128]{1,0:T(8,128)S(1)} %fusion.330, f32[56,128]{1,0:T(8,128)S(1)} %fusion.169, f32[56,128]{1,0:T(8,128)S(1)} %fusion.331, f32[56,128]{1,0:T(8,128)S(1)} %fusion.170, f32[56,128]{1,0:T(8,128)S(1)} %fusion.332, f32[56,128]{1,0:T(8,128)S(1)} %fusion.171, ...), kind=kLoop, calls=%fused_computation.22 | loop fusion | flops 34922496 | bytes 5689600 | tf_op jit(solution)/shard_map/sub | solution.py:109
  459.3 12.7 %multiply_subtract_fusion.11 = f32[56,56,128]{2,0,1:T(8,128)S(1)} fusion(f32[56,128]{1,0:T(8,128)S(1)} %fusion.167, f32[56,128]{1,0:T(8,128)S(1)} %fusion.329, f32[56,128]{1,0:T(8,128)S(1)} %fusion.168, f32[56,128]{1,0:T(8,128)S(1)} %fusion.330, f32[56,128]{1,0:T(8,128)S(1)} %fusion.169, f32[56,128]{1,0:T(8,128)S(1)} %fusion.331, f32[56,128]{1,0:T(8,128)S(1)} %fusion.170, ...), kind=kLoop, calls=%fused_computation.21 | loop fusion | flops 35725312 | bytes 5746944 | tf_op jit(solution)/shard_map/sub | solution.py:109
  473.9 12.8 %multiply_subtract_fusion.10 = f32[56,56,128]{2,0,1:T(8,128)S(1)} fusion(f32[56,128]{1,0:T(8,128)S(1)} %fusion.166, f32[56,128]{1,0:T(8,128)S(1)} %fusion.328, f32[56,128]{1,0:T(8,128)S(1)} %fusion.167, f32[56,128]{1,0:T(8,128)S(1)} %fusion.329, f32[56,128]{1,0:T(8,128)S(1)} %fusion.168, f32[56,128]{1,0:T(8,128)S(1)} %fusion.330, f32[56,128]{1,0:T(8,128)S(1)} %fusion.169, ...), kind=kLoop, calls=%fused_computation.20 | loop fusion | flops 36528128 | bytes 5804288 | tf_op jit(solution)/shard_map/sub | solution.py:109
  488.6 13.1 %multiply_subtract_fusion.9 = f32[56,56,128]{2,0,1:T(8,128)S(1)} fusion(f32[56,128]{1,0:T(8,128)S(1)} %fusion.165, f32[56,128]{1,0:T(8,128)S(1)} %fusion.327, f32[56,128]{1,0:T(8,128)S(1)} %fusion.166, f32[56,128]{1,0:T(8,128)S(1)} %fusion.328, f32[56,128]{1,0:T(8,128)S(1)} %fusion.167, f32[56,128]{1,0:T(8,128)S(1)} %fusion.329, f32[56,128]{1,0:T(8,128)S(1)} %fusion.168, ...), kind=kLoop, calls=%fused_computation.19 | loop fusion | flops 37330944 | bytes 5861632 | tf_op jit(solution)/shard_map/sub | solution.py:109
  502.9 13.8 %multiply_subtract_fusion.8 = f32[56,56,128]{2,0,1:T(8,128)S(1)} fusion(f32[56,128]{1,0:T(8,128)S(1)} %fusion.164, f32[56,128]{1,0:T(8,128)S(1)} %fusion.326, f32[56,128]{1,0:T(8,128)S(1)} %fusion.165, f32[56,128]{1,0:T(8,128)S(1)} %fusion.327, f32[56,128]{1,0:T(8,128)S(1)} %fusion.166, f32[56,128]{1,0:T(8,128)S(1)} %fusion.328, f32[56,128]{1,0:T(8,128)S(1)} %fusion.167, ...), kind=kLoop, calls=%fused_computation.18 | loop fusion | flops 38133760 | bytes 5918976 | tf_op jit(solution)/shard_map/sub | solution.py:109
  517.5 13.7 %multiply_subtract_fusion.7 = f32[56,56,128]{2,0,1:T(8,128)S(1)} fusion(f32[56,128]{1,0:T(8,128)S(1)} %fusion.163, f32[56,128]{1,0:T(8,128)S(1)} %fusion.325, f32[56,128]{1,0:T(8,128)S(1)} %fusion.164, f32[56,128]{1,0:T(8,128)S(1)} %fusion.326, f32[56,128]{1,0:T(8,128)S(1)} %fusion.165, f32[56,128]{1,0:T(8,128)S(1)} %fusion.327, f32[56,128]{1,0:T(8,128)S(1)} %fusion.166, ...), kind=kLoop, calls=%fused_computation.17 | loop fusion | flops 38936576 | bytes 5976320 | tf_op jit(solution)/shard_map/sub | solution.py:109
  532.1 14.0 %multiply_subtract_fusion.6 = f32[56,56,128]{2,0,1:T(8,128)S(1)} fusion(f32[56,128]{1,0:T(8,128)S(1)} %fusion.162, f32[56,128]{1,0:T(8,128)S(1)} %fusion.324, f32[56,128]{1,0:T(8,128)S(1)} %fusion.163, f32[56,128]{1,0:T(8,128)S(1)} %fusion.325, f32[56,128]{1,0:T(8,128)S(1)} %fusion.164, f32[56,128]{1,0:T(8,128)S(1)} %fusion.326, f32[56,128]{1,0:T(8,128)S(1)} %fusion.165, ...), kind=kLoop, calls=%fused_computation.16 | loop fusion | flops 39739392 | bytes 6033664 | tf_op jit(solution)/shard_map/sub | solution.py:109
  547.0 14.5 %multiply_subtract_fusion.5 = f32[56,56,128]{2,0,1:T(8,128)S(1)} fusion(f32[56,128]{1,0:T(8,128)S(1)} %fusion.161, f32[56,128]{1,0:T(8,128)S(1)} %fusion.323, f32[56,128]{1,0:T(8,128)S(1)} %fusion.162, f32[56,128]{1,0:T(8,128)S(1)} %fusion.324, f32[56,128]{1,0:T(8,128)S(1)} %fusion.163, f32[56,128]{1,0:T(8,128)S(1)} %fusion.325, f32[56,128]{1,0:T(8,128)S(1)} %fusion.164, ...), kind=kLoop, calls=%fused_computation.15 | loop fusion | flops 40542208 | bytes 6091008 | tf_op jit(solution)/shard_map/sub | solution.py:109
  562.7 9.3 %multiply_subtract_fusion.4 = f32[56,56,128]{2,0,1:T(8,128)S(1)} fusion(f32[56,128]{1,0:T(8,128)S(1)} %fusion.160, f32[56,128]{1,0:T(8,128)S(1)} %fusion.322, f32[56,128]{1,0:T(8,128)S(1)} %fusion.161, f32[56,128]{1,0:T(8,128)S(1)} %fusion.323, f32[56,128]{1,0:T(8,128)S(1)} %fusion.162, f32[56,128]{1,0:T(8,128)S(1)} %fusion.324, f32[56,128]{1,0:T(8,128)S(1)} %fusion.163, ...), kind=kLoop, calls=%fused_computation.14 | loop fusion | flops 41345024 | bytes 6148352 | tf_op jit(solution)/shard_map/sub | solution.py:109
  572.9 9.9 %multiply_subtract_fusion.3 = f32[56,56,128]{2,0,1:T(8,128)S(1)} fusion(f32[56,128]{1,0:T(8,128)S(1)} %fusion.159, f32[56,128]{1,0:T(8,128)S(1)} %fusion.321, f32[56,128]{1,0:T(8,128)S(1)} %fusion.160, f32[56,128]{1,0:T(8,128)S(1)} %fusion.322, f32[56,128]{1,0:T(8,128)S(1)} %fusion.161, f32[56,128]{1,0:T(8,128)S(1)} %fusion.323, f32[56,128]{1,0:T(8,128)S(1)} %fusion.162, ...), kind=kLoop, calls=%fused_computation.13 | loop fusion | flops 42147840 | bytes 6205696 | tf_op jit(solution)/shard_map/sub | solution.py:109
  583.7 10.6 %multiply_subtract_fusion.2 = f32[56,56,128]{2,0,1:T(8,128)S(1)} fusion(f32[56,128]{1,0:T(8,128)S(1)} %fusion.158, f32[56,128]{1,0:T(8,128)S(1)} %fusion.320, f32[56,128]{1,0:T(8,128)S(1)} %fusion.159, f32[56,128]{1,0:T(8,128)S(1)} %fusion.321, f32[56,128]{1,0:T(8,128)S(1)} %fusion.160, f32[56,128]{1,0:T(8,128)S(1)} %fusion.322, f32[56,128]{1,0:T(8,128)S(1)} %fusion.161, ...), kind=kLoop, calls=%fused_computation.12 | loop fusion | flops 42950656 | bytes 6263040 | tf_op jit(solution)/shard_map/sub | solution.py:109
  595.3 13.5 %multiply_subtract_fusion.1 = f32[56,56,128]{2,0,1:T(8,128)} fusion(f32[56,128]{1,0:T(8,128)S(1)} %fusion.157, f32[56,128]{1,0:T(8,128)S(1)} %fusion.319, f32[56,128]{1,0:T(8,128)S(1)} %fusion.158, f32[56,128]{1,0:T(8,128)S(1)} %fusion.320, f32[56,128]{1,0:T(8,128)S(1)} %fusion.159, f32[56,128]{1,0:T(8,128)S(1)} %fusion.321, f32[56,128]{1,0:T(8,128)S(1)} %fusion.160, ...), kind=kLoop, calls=%fused_computation.11 | loop fusion | flops 43753472 | bytes 6320384 | tf_op jit(solution)/shard_map/sub | solution.py:109
  650.2 11.0 %multiply_subtract_fusion = f32[56,56,128]{2,0,1:T(8,128)S(1)} fusion(f32[56,128]{1,0:T(8,128)S(1)} %fusion.156, f32[56,128]{1,0:T(8,128)S(1)} %fusion.318, f32[56,128]{1,0:T(8,128)S(1)} %fusion.157, f32[56,128]{1,0:T(8,128)S(1)} %fusion.319, f32[56,128]{1,0:T(8,128)S(1)} %fusion.158, f32[56,128]{1,0:T(8,128)S(1)} %fusion.320, f32[56,128]{1,0:T(8,128)S(1)} %fusion.159, ...), kind=kLoop, calls=%fused_computation.10 | loop fusion | flops 44556288 | bytes 6377728 | tf_op jit(solution)/shard_map/sub | solution.py:109
  663.5 5.0 stack.20
  668.6 12.3 %stack.21 = f32[56,56,128]{2,1,0:T(8,128)} concatenate(f32[56,1,128]{2,1,0:T(1,128)} %bitcast.1360, f32[56,1,128]{2,1,0:T(1,128)S(1)} %bitcast.1306, f32[56,1,128]{2,1,0:T(1,128)S(1)} %bitcast.1307, f32[56,1,128]{2,1,0:T(1,128)S(1)} %bitcast.1308, f32[56,1,128]{2,1,0:T(1,128)S(1)} %bitcast.1309, f32[56,1,128]{2,1,0:T(1,128)S(1)} %bitcast.1310, f32[56,1,128]{2,1,0:T(1,128)S(1)} %bitcast.1311, ...), dimensions={1} | concatenate | bytes 3211264 | tf_op jit(solution)/shard_map/stack | solution.py:110
  696.8 4.3 stack.22
  710.5 58.1 %all-gather.2.cloned.1.call-done = f32[56,16384]{1,0:T(8,128)} async-done(((f32[56,128]{1,0:T(8,128)}), f32[56,16384]{1,0:T(8,128)}) %all-gather.2.cloned.1.call-update) | async-done | bytes 3670032 | tf_op jit(solution)/shard_map/all_gather | solution.py:209
  768.6 6.7 copy.1028
  775.3 4.0 gather_fusion.1
  779.5 1.8 fusion.6
  781.3 1.8 fusion.8
  (1187 shorter events, 213.9 us)
Async XLA Ops:
  55.1 86.1 %all-to-all-start = ((f32[32,4,2432]{2,1,0:T(4,128)}), f32[32,4,2432]{2,1,0:T(4,128)S(1)}, u32[]{:S(2)}, u32[]{:S(2)}) async-start(f32[32,4,2432]{2,1,0:T(4,128)} %all_to_all.8), calls=%async_computation | async-start | bytes 2490368 | tf_op jit(solution)/shard_map/all_to_all | solution.py:203
  64.8 145.3 %reduce-scatter.2.cloned.1.call-start = ((), (), s32[]{:S(2)}) async-start(), calls=%async_computation.2 | async-start | bytes 6225920 | tf_op jit(solution)/shard_map/reduce_scatter | solution.py:206
  160.4 608.2 %all-gather.2.cloned.1.call-start = ((), (), s32[]{:S(2)}) async-start(), calls=%async_computation.3 | async-start | bytes 3698688 | tf_op jit(solution)/shard_map/all_gather | solution.py:209
  161.8 50.8 %copy-start.61 = (f32[6,189]{1,0:T(8,128)}, f32[6,189]{1,0:T(8,128)S(1)}, u32[]{:S(2)}) copy-start(f32[6,189]{1,0:T(8,128)S(1)} %fusion.226) | copy-start | bytes 13612
  161.9 50.8 %copy-start.63 = (f32[6,189]{1,0:T(8,128)}, f32[6,189]{1,0:T(8,128)S(1)}, u32[]{:S(2)}) copy-start(f32[6,189]{1,0:T(8,128)S(1)} %fusion.376) | copy-start | bytes 13612
  162.7 50.0 %copy-start.181 = (pred[6]{0:T(512)(128)(4,1)}, pred[6]{0:T(512)(128)(4,1)S(1)}, u32[]{:S(2)}) copy-start(pred[6]{0:T(512)(128)(4,1)S(1)} %iota_compare_fusion.6) | copy-start | bytes 22
  162.9 49.7 %copy-start.91 = (f32[1,1,189]{2,0,1:T(1,128)}, f32[1,1,189]{2,0,1:T(1,128)S(1)}, u32[]{:S(2)}) copy-start(f32[1,1,189]{2,0,1:T(1,128)S(1)} %slice_sqrt_fusion.2) | copy-start | bytes 2272
  163.6 57.6 %copy-start.175 = (pred[56]{0:T(512)(128)(4,1)}, pred[56]{0:T(512)(128)(4,1)S(1)}, u32[]{:S(2)}) copy-start(pred[56]{0:T(512)(128)(4,1)S(1)} %iota_compare_fusion.63) | copy-start | bytes 172
  163.6 58.8 %copy-start.173 = (pred[56]{0:T(512)(128)(4,1)}, pred[56]{0:T(512)(128)(4,1)S(1)}, u32[]{:S(2)}) copy-start(pred[56]{0:T(512)(128)(4,1)S(1)} %iota_compare_fusion.62) | copy-start | bytes 172
  163.7 59.7 %copy-start.171 = (pred[56]{0:T(512)(128)(4,1)}, pred[56]{0:T(512)(128)(4,1)S(1)}, u32[]{:S(2)}) copy-start(pred[56]{0:T(512)(128)(4,1)S(1)} %iota_compare_fusion.61) | copy-start | bytes 172
  163.7 61.7 %copy-start.169 = (pred[56]{0:T(512)(128)(4,1)}, pred[56]{0:T(512)(128)(4,1)S(1)}, u32[]{:S(2)}) copy-start(pred[56]{0:T(512)(128)(4,1)S(1)} %iota_compare_fusion.60) | copy-start | bytes 172
  163.7 63.8 %copy-start.167 = (pred[56]{0:T(512)(128)(4,1)}, pred[56]{0:T(512)(128)(4,1)S(1)}, u32[]{:S(2)}) copy-start(pred[56]{0:T(512)(128)(4,1)S(1)} %iota_compare_fusion.59) | copy-start | bytes 172
  163.7 66.0 %copy-start.165 = (pred[56]{0:T(512)(128)(4,1)}, pred[56]{0:T(512)(128)(4,1)S(1)}, u32[]{:S(2)}) copy-start(pred[56]{0:T(512)(128)(4,1)S(1)} %iota_compare_fusion.58) | copy-start | bytes 172
  163.7 68.3 %copy-start.163 = (pred[56]{0:T(512)(128)(4,1)}, pred[56]{0:T(512)(128)(4,1)S(1)}, u32[]{:S(2)}) copy-start(pred[56]{0:T(512)(128)(4,1)S(1)} %iota_compare_fusion.57) | copy-start | bytes 172
  163.8 70.6 %copy-start.161 = (pred[56]{0:T(512)(128)(4,1)}, pred[56]{0:T(512)(128)(4,1)S(1)}, u32[]{:S(2)}) copy-start(pred[56]{0:T(512)(128)(4,1)S(1)} %iota_compare_fusion.56) | copy-start | bytes 172
  163.8 73.1 %copy-start.159 = (pred[56]{0:T(512)(128)(4,1)}, pred[56]{0:T(512)(128)(4,1)S(1)}, u32[]{:S(2)}) copy-start(pred[56]{0:T(512)(128)(4,1)S(1)} %iota_compare_fusion.55) | copy-start | bytes 172
  163.8 75.6 %copy-start.157 = (pred[56]{0:T(512)(128)(4,1)}, pred[56]{0:T(512)(128)(4,1)S(1)}, u32[]{:S(2)}) copy-start(pred[56]{0:T(512)(128)(4,1)S(1)} %iota_compare_fusion.54) | copy-start | bytes 172
  163.8 78.5 %copy-start.155 = (pred[56]{0:T(512)(128)(4,1)}, pred[56]{0:T(512)(128)(4,1)S(1)}, u32[]{:S(2)}) copy-start(pred[56]{0:T(512)(128)(4,1)S(1)} %iota_compare_fusion.53) | copy-start | bytes 172
  163.9 81.2 %copy-start.153 = (pred[56]{0:T(512)(128)(4,1)}, pred[56]{0:T(512)(128)(4,1)S(1)}, u32[]{:S(2)}) copy-start(pred[56]{0:T(512)(128)(4,1)S(1)} %iota_compare_fusion.52) | copy-start | bytes 172
  163.9 84.1 %copy-start.151 = (pred[56]{0:T(512)(128)(4,1)}, pred[56]{0:T(512)(128)(4,1)S(1)}, u32[]{:S(2)}) copy-start(pred[56]{0:T(512)(128)(4,1)S(1)} %iota_compare_fusion.51) | copy-start | bytes 172
  163.9 87.1 %copy-start.149 = (pred[56]{0:T(512)(128)(4,1)}, pred[56]{0:T(512)(128)(4,1)S(1)}, u32[]{:S(2)}) copy-start(pred[56]{0:T(512)(128)(4,1)S(1)} %iota_compare_fusion.50) | copy-start | bytes 172
  163.9 90.1 %copy-start.147 = (pred[56]{0:T(512)(128)(4,1)}, pred[56]{0:T(512)(128)(4,1)S(1)}, u32[]{:S(2)}) copy-start(pred[56]{0:T(512)(128)(4,1)S(1)} %iota_compare_fusion.49) | copy-start | bytes 172
  163.9 93.4 %copy-start.145 = (pred[56]{0:T(512)(128)(4,1)}, pred[56]{0:T(512)(128)(4,1)S(1)}, u32[]{:S(2)}) copy-start(pred[56]{0:T(512)(128)(4,1)S(1)} %iota_compare_fusion.48) | copy-start | bytes 172
  164.0 97.6 %copy-start.143 = (pred[56]{0:T(512)(128)(4,1)}, pred[56]{0:T(512)(128)(4,1)S(1)}, u32[]{:S(2)}) copy-start(pred[56]{0:T(512)(128)(4,1)S(1)} %iota_compare_fusion.47) | copy-start | bytes 172
  164.0 100.9 %copy-start.141 = (pred[56]{0:T(512)(128)(4,1)}, pred[56]{0:T(512)(128)(4,1)S(1)}, u32[]{:S(2)}) copy-start(pred[56]{0:T(512)(128)(4,1)S(1)} %iota_compare_fusion.46) | copy-start | bytes 172
  164.0 104.2 %copy-start.139 = (pred[56]{0:T(512)(128)(4,1)}, pred[56]{0:T(512)(128)(4,1)S(1)}, u32[]{:S(2)}) copy-start(pred[56]{0:T(512)(128)(4,1)S(1)} %iota_compare_fusion.45) | copy-start | bytes 172
  164.0 107.6 %copy-start.137 = (pred[56]{0:T(512)(128)(4,1)}, pred[56]{0:T(512)(128)(4,1)S(1)}, u32[]{:S(2)}) copy-start(pred[56]{0:T(512)(128)(4,1)S(1)} %iota_compare_fusion.44) | copy-start | bytes 172
  164.1 111.1 %copy-start.135 = (pred[56]{0:T(512)(128)(4,1)}, pred[56]{0:T(512)(128)(4,1)S(1)}, u32[]{:S(2)}) copy-start(pred[56]{0:T(512)(128)(4,1)S(1)} %iota_compare_fusion.43) | copy-start | bytes 172
  164.1 115.1 %copy-start.133 = (pred[56]{0:T(512)(128)(4,1)}, pred[56]{0:T(512)(128)(4,1)S(1)}, u32[]{:S(2)}) copy-start(pred[56]{0:T(512)(128)(4,1)S(1)} %iota_compare_fusion.42) | copy-start | bytes 172
  164.1 118.9 %copy-start.131 = (pred[56]{0:T(512)(128)(4,1)}, pred[56]{0:T(512)(128)(4,1)S(1)}, u32[]{:S(2)}) copy-start(pred[56]{0:T(512)(128)(4,1)S(1)} %iota_compare_fusion.41) | copy-start | bytes 172
  164.1 123.9 %copy-start.129 = (pred[56]{0:T(512)(128)(4,1)}, pred[56]{0:T(512)(128)(4,1)S(1)}, u32[]{:S(2)}) copy-start(pred[56]{0:T(512)(128)(4,1)S(1)} %iota_compare_fusion.40) | copy-start | bytes 172
  164.1 129.1 %copy-start.127 = (pred[56]{0:T(512)(128)(4,1)}, pred[56]{0:T(512)(128)(4,1)S(1)}, u32[]{:S(2)}) copy-start(pred[56]{0:T(512)(128)(4,1)S(1)} %iota_compare_fusion.39) | copy-start | bytes 172
  164.2 134.7 %copy-start.125 = (pred[56]{0:T(512)(128)(4,1)}, pred[56]{0:T(512)(128)(4,1)S(1)}, u32[]{:S(2)}) copy-start(pred[56]{0:T(512)(128)(4,1)S(1)} %iota_compare_fusion.38) | copy-start | bytes 172
  595.3 26.1 %copy-start.156 = (pred[56]{0:T(512)(128)(4,1)S(1)}, pred[56]{0:T(512)(128)(4,1)}, u32[]{:S(2)}) copy-start(pred[56]{0:T(512)(128)(4,1)} %copy-done.155) | copy-start | bytes 172
  595.3 27.0 %copy-start.154 = (pred[56]{0:T(512)(128)(4,1)S(1)}, pred[56]{0:T(512)(128)(4,1)}, u32[]{:S(2)}) copy-start(pred[56]{0:T(512)(128)(4,1)} %copy-done.153) | copy-start | bytes 172
  595.3 27.8 %copy-start.152 = (pred[56]{0:T(512)(128)(4,1)S(1)}, pred[56]{0:T(512)(128)(4,1)}, u32[]{:S(2)}) copy-start(pred[56]{0:T(512)(128)(4,1)} %copy-done.151) | copy-start | bytes 172
  595.3 28.7 %copy-start.150 = (pred[56]{0:T(512)(128)(4,1)S(1)}, pred[56]{0:T(512)(128)(4,1)}, u32[]{:S(2)}) copy-start(pred[56]{0:T(512)(128)(4,1)} %copy-done.149) | copy-start | bytes 172
  595.3 29.5 %copy-start.148 = (pred[56]{0:T(512)(128)(4,1)S(1)}, pred[56]{0:T(512)(128)(4,1)}, u32[]{:S(2)}) copy-start(pred[56]{0:T(512)(128)(4,1)} %copy-done.147) | copy-start | bytes 172
  613.5 26.6 %copy-start.186 = (f32[1,128]{1,0:T(1,128)}, f32[1,128]{1,0:T(1,128)S(1)}, u32[]{:S(2)}) copy-start(f32[1,128]{1,0:T(1,128)S(1)} %slice_divide_fusion.120) | copy-start | bytes 1540
  614.3 26.6 %copy-start.187 = (f32[1,128]{1,0:T(1,128)}, f32[1,128]{1,0:T(1,128)S(1)}, u32[]{:S(2)}) copy-start(f32[1,128]{1,0:T(1,128)S(1)} %slice_divide_fusion.119) | copy-start | bytes 1540
  614.4 27.3 %copy-start.188 = (f32[1,128]{1,0:T(1,128)}, f32[1,128]{1,0:T(1,128)S(1)}, u32[]{:S(2)}) copy-start(f32[1,128]{1,0:T(1,128)S(1)} %slice_divide_fusion.118) | copy-start | bytes 1540
  615.3 27.3 %copy-start.189 = (f32[1,128]{1,0:T(1,128)}, f32[1,128]{1,0:T(1,128)S(1)}, u32[]{:S(2)}) copy-start(f32[1,128]{1,0:T(1,128)S(1)} %slice_divide_fusion.117) | copy-start | bytes 1540
  616.2 27.3 %copy-start.190 = (f32[1,128]{1,0:T(1,128)}, f32[1,128]{1,0:T(1,128)S(1)}, u32[]{:S(2)}) copy-start(f32[1,128]{1,0:T(1,128)S(1)} %slice_divide_fusion.116) | copy-start | bytes 1540
  617.0 27.3 %copy-start.191 = (f32[1,128]{1,0:T(1,128)}, f32[1,128]{1,0:T(1,128)S(1)}, u32[]{:S(2)}) copy-start(f32[1,128]{1,0:T(1,128)S(1)} %slice_divide_fusion.115) | copy-start | bytes 1540
  617.9 27.3 %copy-start.192 = (f32[1,128]{1,0:T(1,128)}, f32[1,128]{1,0:T(1,128)S(1)}, u32[]{:S(2)}) copy-start(f32[1,128]{1,0:T(1,128)S(1)} %slice_divide_fusion.114) | copy-start | bytes 1540
  618.8 27.3 %copy-start.193 = (f32[1,128]{1,0:T(1,128)}, f32[1,128]{1,0:T(1,128)S(1)}, u32[]{:S(2)}) copy-start(f32[1,128]{1,0:T(1,128)S(1)} %slice_divide_fusion.113) | copy-start | bytes 1540
  619.6 27.3 %copy-start.194 = (f32[1,128]{1,0:T(1,128)}, f32[1,128]{1,0:T(1,128)S(1)}, u32[]{:S(2)}) copy-start(f32[1,128]{1,0:T(1,128)S(1)} %slice_divide_fusion.112) | copy-start | bytes 1540
  620.5 27.3 %copy-start.195 = (f32[1,128]{1,0:T(1,128)}, f32[1,128]{1,0:T(1,128)S(1)}, u32[]{:S(2)}) copy-start(f32[1,128]{1,0:T(1,128)S(1)} %slice_divide_fusion.111) | copy-start | bytes 1540
  621.4 27.3 %copy-start.196 = (f32[1,128]{1,0:T(1,128)}, f32[1,128]{1,0:T(1,128)S(1)}, u32[]{:S(2)}) copy-start(f32[1,128]{1,0:T(1,128)S(1)} %slice_divide_fusion.110) | copy-start | bytes 1540
  622.2 26.6 %copy-start.197 = (f32[1,128]{1,0:T(1,128)}, f32[1,128]{1,0:T(1,128)S(1)}, u32[]{:S(2)}) copy-start(f32[1,128]{1,0:T(1,128)S(1)} %slice_divide_fusion.109) | copy-start | bytes 1540
  627.5 33.7 %copy-start.204 = (f32[1,128]{1,0:T(1,128)}, f32[1,128]{1,0:T(1,128)S(1)}, u32[]{:S(2)}) copy-start(f32[1,128]{1,0:T(1,128)S(1)} %slice_divide_fusion.102) | copy-start | bytes 1540
  627.6 33.6 %copy-start.205 = (f32[1,128]{1,0:T(1,128)}, f32[1,128]{1,0:T(1,128)S(1)}, u32[]{:S(2)}) copy-start(f32[1,128]{1,0:T(1,128)S(1)} %slice_divide_fusion.101) | copy-start | bytes 1540
  627.8 33.5 %copy-start.206 = (f32[1,128]{1,0:T(1,128)}, f32[1,128]{1,0:T(1,128)S(1)}, u32[]{:S(2)}) copy-start(f32[1,128]{1,0:T(1,128)S(1)} %slice_divide_fusion.100) | copy-start | bytes 1540
  627.9 33.4 %copy-start.207 = (f32[1,128]{1,0:T(1,128)}, f32[1,128]{1,0:T(1,128)S(1)}, u32[]{:S(2)}) copy-start(f32[1,128]{1,0:T(1,128)S(1)} %slice_divide_fusion.99) | copy-start | bytes 1540
  628.0 33.3 %copy-start.208 = (f32[1,128]{1,0:T(1,128)}, f32[1,128]{1,0:T(1,128)S(1)}, u32[]{:S(2)}) copy-start(f32[1,128]{1,0:T(1,128)S(1)} %slice_divide_fusion.98) | copy-start | bytes 1540
  628.9 32.5 %copy-start.209 = (f32[1,128]{1,0:T(1,128)}, f32[1,128]{1,0:T(1,128)S(1)}, u32[]{:S(2)}) copy-start(f32[1,128]{1,0:T(1,128)S(1)} %slice_divide_fusion.97) | copy-start | bytes 1540
  629.7 31.6 %copy-start.210 = (f32[1,128]{1,0:T(1,128)}, f32[1,128]{1,0:T(1,128)S(1)}, u32[]{:S(2)}) copy-start(f32[1,128]{1,0:T(1,128)S(1)} %slice_divide_fusion.96) | copy-start | bytes 1540
  630.6 30.8 %copy-start.211 = (f32[1,128]{1,0:T(1,128)}, f32[1,128]{1,0:T(1,128)S(1)}, u32[]{:S(2)}) copy-start(f32[1,128]{1,0:T(1,128)S(1)} %slice_divide_fusion.95) | copy-start | bytes 1540
  631.5 29.9 %copy-start.212 = (f32[1,128]{1,0:T(1,128)}, f32[1,128]{1,0:T(1,128)S(1)}, u32[]{:S(2)}) copy-start(f32[1,128]{1,0:T(1,128)S(1)} %slice_divide_fusion.94) | copy-start | bytes 1540
  632.3 29.1 %copy-start.213 = (f32[1,128]{1,0:T(1,128)}, f32[1,128]{1,0:T(1,128)S(1)}, u32[]{:S(2)}) copy-start(f32[1,128]{1,0:T(1,128)S(1)} %slice_divide_fusion.93) | copy-start | bytes 1540
  633.2 28.2 %copy-start.214 = (f32[1,128]{1,0:T(1,128)}, f32[1,128]{1,0:T(1,128)S(1)}, u32[]{:S(2)}) copy-start(f32[1,128]{1,0:T(1,128)S(1)} %slice_divide_fusion.92) | copy-start | bytes 1540
  634.0 27.4 %copy-start.215 = (f32[1,128]{1,0:T(1,128)}, f32[1,128]{1,0:T(1,128)S(1)}, u32[]{:S(2)}) copy-start(f32[1,128]{1,0:T(1,128)S(1)} %slice_divide_fusion.91) | copy-start | bytes 1540
  634.9 26.5 %copy-start.216 = (f32[1,128]{1,0:T(1,128)}, f32[1,128]{1,0:T(1,128)S(1)}, u32[]{:S(2)}) copy-start(f32[1,128]{1,0:T(1,128)S(1)} %slice_divide_fusion.90) | copy-start | bytes 1540
  707.3 68.0 %copy-start.84 = (f32[6,189]{1,0:T(8,128)}, f32[6,189]{1,0:T(8,128)S(1)}, u32[]{:S(2)}) copy-start(f32[6,189]{1,0:T(8,128)S(1)} %stack.26) | copy-start | bytes 13612
  (184 other events, 1783.1 us)
Sparse Core Ops, SparseCore 0:
  160.5 49.5 reduce-scatter.1
  701.2 67.2 all-gather.1
where the time goes:
time: 806 us; the launch traced here: 791 us
  other arithmetic  458 us (57%)
  local copies, waits for them, and re-layouts  117 us (15%)
  waiting for transfers between devices  87.4 us (11%)
  blocking collectives  67.1 us (8%)
  matrix products  30.4 us (4%)
  between operations  20.7 us (3%)
  starting transfers between devices  10.4 us (1%)
    sub x60, other arithmetic, batched_cholesky_solve(): work = work - column[:, None, :] * column[None, :, :]  324 us
    psum x1, blocking collectives, shards(): ccd_table = lax.psum(ccd_local, ('field', 'shard'))  67.1 us
    all_gather x1, waiting for transfers between devices, shards(): lax.all_gather(exposure_update, ('field', 'shard'), axis=1, tiled=True)  58.1 us
    unnamed x494, local copies, waits for them, and re-layouts  44.7 us
    sub x58, other arithmetic, batched_cholesky_solve(): remain = remain - lower[:, step] * value[None, :]  38.8 us
    select_n x118, other arithmetic, batched_cholesky_solve(): column = jnp.where((rows_idx >= step)[:, None], column, jnp.float32(0.0))  35.6 us
    reduce_scatter x1, waiting for transfers between devices, shards(): summed = lax.psum_scatter(table, 'field', scatter_dimension=0, tiled=True)  29.3 us
    dot_general x6, matrix products, outer(): jnp.einsum('...ps,...qs->...pq', basis * scale[..., None, :], basis, prec...  17.7 us
  transfers between devices with their start and end apart: 3, of which 2 were waited for; matrix products, arithmetic and copies ran while one was open for 5% of the time, Pallas kernels for 0%

commit v1 on v0

v1 whole, which is shorter than its diff:
```python
import math

import jax
import jax.numpy as jnp
import numpy as np
from jax import lax
from jax.experimental import pallas as pl
from jax.experimental.pallas import tpu as pltpu
from jax.sharding import PartitionSpec as P

ORDER = 6
POLY = 28
VISITS = 6
NCCD = 189
LANES = 128
STAR_DAMP = 0.1
EXPOSURE_DAMP = 1.0
DETECTOR_DAMP = 1.0
HIGH = lax.Precision.HIGHEST
DEG2 = 2 * ORDER
F32 = jnp.float32

TERMS = [(i, n - i) for n in range(DEG2 + 1) for i in range(n + 1)]
TERM_INDEX = {term: at for at, term in enumerate(TERMS)}
SCALE = [math.sqrt((2 * i + 1) * (2 * j + 1)) for i, j in TERMS[:POLY]]

ROW_GX = 288
ROW_GY = 320
ROW_DET = 352
ROWS = 384
MARK = 95


def linearisation():
    from numpy.polynomial import legendre

    table = np.zeros((ORDER + 1, ORDER + 1, DEG2 + 1))
    for m in range(ORDER + 1):
        for n in range(ORDER + 1):
            product = legendre.legmul([0] * m + [1], [0] * n + [1])
            table[m, n, : len(product)] = product
    return table


def expansion():
    table = linearisation()
    matrix = np.zeros((POLY * 32, 96))
    for q, (iq, jq) in enumerate(TERMS[:POLY]):
        for p, (ip, jp) in enumerate(TERMS[:POLY]):
            for at, (a, b) in enumerate(TERMS):
                matrix[q * 32 + p, at] = SCALE[p] * SCALE[q] * table[ip, iq, a] * table[jp, jq, b]
    return matrix.astype(np.float32)


def scale_rows():
    rows = np.zeros((32, LANES), np.float32)
    rows[:POLY] = np.array(SCALE, np.float32)[:, None]
    return rows


def dot(a, b, dims):
    return lax.dot_general(a, b, (dims, ((), ())), precision=HIGH, preferred_element_type=F32)


def iota(shape, axis):
    return lax.broadcasted_iota(jnp.int32, shape, axis)


def legendre(value, count):
    values = [None, value]
    for degree in range(1, count - 1):
        lower = (degree / (degree + 1)) * (values[degree - 1] if degree > 1 else 1.0)
        values.append(((2 * degree + 1) / (degree + 1)) * value * values[degree] - lower)
    return values


def star_terms(uv_ref, off_ref, diag_ref, corr_ref, count_ref):
    tiles = corr_ref.shape[0]
    lanes = iota((tiles, LANES), 1)
    counts = jnp.broadcast_to(count_ref[...].astype(F32), (tiles, tiles))
    square = (iota((tiles, tiles), 0) == iota((tiles, tiles), 1)).astype(F32)
    column = jnp.sum(counts * square, axis=1, keepdims=True)
    present = (lanes.astype(F32) < column).astype(F32)

    def rows(ref, visit, part):
        return ref[pl.ds(2 * visit + part, tiles, stride=2 * VISITS), :]

    weights = []
    resid = []
    for visit in range(VISITS):
        d0 = rows(diag_ref, visit, 0)
        d1 = rows(diag_ref, visit, 1)
        weights.append((d0 * present, d1 * present, corr_ref[:, visit, :] * jnp.sqrt(d0 * d1) * present))
        resid.append((rows(off_ref, visit, 0), rows(off_ref, visit, 1)))
    hess_xx = sum(w[0] for w in weights) + STAR_DAMP
    hess_yy = sum(w[1] for w in weights) + STAR_DAMP
    hess_xy = sum(w[2] for w in weights)
    determ = hess_xx * hess_yy - hess_xy * hess_xy
    inverse = (hess_yy / determ, hess_xx / determ, -hess_xy / determ)
    return weights, resid, inverse


def apply_inverse(inverse, x, y):
    inv_xx, inv_yy, inv_xy = inverse
    return inv_xx * x + inv_xy * y, inv_xy * x + inv_yy * y


def combine(values, sub):
    for shift in (4, 2, 1):
        low = (sub & shift) == 0
        half = len(values) // 2
        merged = []
        for at in range(half):
            a, b = values[at], values[at + half]
            if shift == 4:
                merged.append(jnp.where(low, a, b) + pltpu.roll(jnp.where(low, b, a), 4, 0))
            else:
                merged.append(jnp.where(low, a + pltpu.roll(a, 8 - shift, 0), b + pltpu.roll(b, shift, 0)))
        values = merged
    return values[0]


def transpose8(values, sub):
    values = list(values)
    for shift in (4, 2, 1):
        low = (sub & shift) == 0
        for at in range(8):
            if at & shift:
                continue
            a, b = values[at], values[at + shift]
            values[at] = jnp.where(low, a, pltpu.roll(b, shift, 0))
            values[at + shift] = jnp.where(low, pltpu.roll(a, 8 - shift, 0), b)
    return values


def moments_kernel(uv_ref, off_ref, diag_ref, corr_ref, count_ref, ids_ref, ccd_ref, slot_ref,
                   out_ref, uvt_ref, where_ref, chan, pu, pv, acc, mom):
    tiles = corr_ref.shape[0]
    visits_all = tiles * VISITS
    sub8 = iota((8, LANES), 0)

    lane16 = iota((tiles, LANES), 1)
    pad = jnp.zeros((LANES - visits_all, LANES), F32)
    ids = [
        jnp.where(lane16 < 64, ids_ref[:, k : k + 1], ccd_ref[:, k : k + 1]).astype(F32)
        for k in range(VISITS)
    ]
    turned = jnp.concatenate(ids + [pad], axis=0).T
    ident = turned[0:1].astype(jnp.int32)
    ccd = turned[64:65].astype(jnp.int32)
    rows128 = iota((LANES, LANES), 0)
    lanes128 = iota((LANES, LANES), 1)
    valid = iota((1, LANES), 1) < visits_all
    picked = dot(slot_ref[...].astype(F32), (rows128 == ident // LANES).astype(F32), ((0,), (0,)))
    position = jnp.sum(jnp.where(rows128 == ident % LANES, picked, 0.0), axis=0, keepdims=True)
    position = (position + 0.5).astype(jnp.int32)
    dest = jnp.where(valid, position // LANES, -1)
    ccd = jnp.where(valid, ccd, -2)
    dest_t = jnp.broadcast_to(dest.astype(F32), (LANES, LANES)).T.astype(jnp.int32)
    same = (dest_t == dest) & (rows128 < lanes128)
    copy_at = jnp.sum(same.astype(F32), axis=0, keepdims=True).astype(jnp.int32)
    mark = (position % LANES + 1).astype(F32)
    where_ref[...] = jnp.where(sub8 == 0, dest, jnp.where(sub8 == 1, copy_at, ccd))

    weights, resid, inverse = star_terms(uv_ref, off_ref, diag_ref, corr_ref, count_ref)
    grad_x = sum(w[0] * r[0] + w[2] * r[1] for w, r in zip(weights, resid))
    grad_y = sum(w[2] * r[0] + w[1] * r[1] for w, r in zip(weights, resid))
    shift_x, shift_y = apply_inverse(inverse, grad_x, grad_y)
    inv_xx, inv_yy, inv_xy = inverse
    channels = [[] for _ in range(7)]
    for visit in range(VISITS):
        w_xx, w_yy, w_xy = weights[visit]
        left_x = resid[visit][0] - shift_x
        left_y = resid[visit][1] - shift_y
        prod_11 = inv_xx * w_xx + inv_xy * w_xy
        prod_12 = inv_xx * w_xy + inv_xy * w_yy
        prod_21 = inv_xy * w_xx + inv_yy * w_xy
        prod_22 = inv_xy * w_xy + inv_yy * w_yy
        values = (
            uv_ref[pl.ds(2 * visit, tiles, stride=2 * VISITS), :],
            uv_ref[pl.ds(2 * visit + 1, tiles, stride=2 * VISITS), :],
            w_xx - (w_xx * prod_11 + w_xy * prod_21),
            w_yy - (w_xy * prod_12 + w_yy * prod_22),
            w_xy - (w_xx * prod_12 + w_xy * prod_22),
            w_xx * left_x + w_xy * left_y,
            w_xy * left_x + w_yy * left_y,
        )
        for at, value in enumerate(values):
            channels[at].append(value)
    for at in range(7):
        chan[at] = jnp.concatenate(channels[at] + [pad], axis=0).T
    uvt_ref[0] = chan[0]
    uvt_ref[1] = chan[1]

    groups = LANES // 8

    def tables(g, carry):
        at = pl.ds(pl.multiple_of(g * 8, 8), 8)
        for ref, source in ((pu, 0), (pv, 1)):
            for degree, value in enumerate(legendre(chan[source, at, :], DEG2 + 1)):
                if degree:
                    ref[degree, at, :] = value
        return carry

    lax.fori_loop(0, groups, tables, 0)

    def sweep(i, top, first, count, row0, width):
        heights = top - i + 1

        def step(g, carry):
            at = pl.ds(pl.multiple_of(g * 8, 8), 8)
            scaled = [chan[first + w, at, :] for w in range(count)]
            if i:
                factor = pu[i, at, :]
                scaled = [value * factor for value in scaled]
            new = []
            for j in range(heights):
                other = pv[j, at, :] if j else None
                for w in range(count):
                    term = scaled[w] * other if j else scaled[w]
                    new.append(carry[j * count + w] + term)
            return tuple(new)

        start = tuple(jnp.zeros((8, LANES), F32) for _ in range(heights * count))
        sums = lax.fori_loop(0, groups, step, start, unroll=2)
        for j in range(heights):
            for w in range(count):
                row = row0 + w * width + TERM_INDEX[(i, j)]
                acc[pl.ds(row * 8, 8), :] = sums[j * count + w]

    for i in range(DEG2 + 1):
        sweep(i, DEG2, 2, 3, 0, 96)
    for i in range(ORDER + 1):
        sweep(i, ORDER, 5, 2, ROW_GX, 32)
    zero = jnp.zeros((8, LANES), F32)
    for block in range(3):
        for row in range(len(TERMS), 96):
            acc[pl.ds((block * 96 + row) * 8, 8), :] = zero
    for block in range(2):
        for row in range(POLY, 32):
            acc[pl.ds((ROW_GX + block * 32 + row) * 8, 8), :] = zero

    def reduce_rows(g, carry):
        base = pl.multiple_of(g * 64, 64)
        mom[pl.ds(pl.multiple_of(g * 8, 8), 8), :] = combine(
            [acc[pl.ds(base + 8 * s, 8), :] for s in range(8)], sub8
        )
        return carry

    lax.fori_loop(0, ROW_DET // 8, reduce_rows, 0, unroll=2)
    mom[88:96, :] = jnp.where(sub8 == 7, mark, mom[88:96, :])

    zeros96 = jnp.zeros((96, LANES), F32)
    pulls = jnp.where(sub8 < 4, mom[ROW_GX : ROW_GX + 8], pltpu.roll(mom[ROW_GY : ROW_GY + 8], 4, 0))
    last = jnp.concatenate(
        [
            jnp.concatenate([mom[256:352], jnp.zeros((32, LANES), F32)], axis=0),
            jnp.concatenate([zeros96, mom[0:8], mom[96:104], mom[192:200], pulls], axis=0),
        ],
        axis=1,
    )
    for copy in range(2):
        place = ((rows128 == dest) & (copy_at == copy)).astype(F32)
        place_det = (rows128 * 2 + copy == ccd).astype(F32)
        out_ref[:, 3 * copy, :] = dot(place, mom[0:128], ((1,), (1,)))
        out_ref[:, 3 * copy + 1, :] = dot(place, mom[128:256], ((1,), (1,)))
        out_ref[:, 3 * copy + 2, :] = dot(
            jnp.concatenate([place, place_det], axis=1), last, ((1,), (1,))
        )


def detector_solve(table):
    def moment(block, i, j):
        return table[8 * block + TERM_INDEX[(i, j)] : 8 * block + TERM_INDEX[(i, j)] + 1]

    def block_of(block):
        one, u, v = moment(block, 0, 0), moment(block, 1, 0), moment(block, 0, 1)
        uu = (2.0 * moment(block, 2, 0) + one) * (1.0 / 3.0)
        vv = (2.0 * moment(block, 0, 2) + one) * (1.0 / 3.0)
        uv = moment(block, 1, 1)
        return [[one, u, v], [u, uu, uv], [v, uv, vv]]

    part_xx, part_yy, part_xy = block_of(0), block_of(1), block_of(2)
    matrix = [part_xx[p] + part_xy[p] for p in range(3)] + [part_xy[p] + part_yy[p] for p in range(3)]
    at = [TERM_INDEX[term] for term in ((0, 0), (1, 0), (0, 1))]
    rhs = [table[24 + a : 25 + a] for a in at] + [table[28 + a : 29 + a] for a in at]
    for p in range(6):
        matrix[p][p] = matrix[p][p] + DETECTOR_DAMP
    inverse = [None] * 6
    lower = [[None] * 6 for _ in range(6)]
    for step in range(6):
        pivot = matrix[step][step]
        for before in range(step):
            pivot = pivot - lower[step][before] * lower[step][before]
        inverse[step] = 1.0 / jnp.sqrt(pivot)
        for row in range(step + 1, 6):
            value = matrix[row][step]
            for before in range(step):
                value = value - lower[row][before] * lower[step][before]
            lower[row][step] = value * inverse[step]
    forward = []
    for step in range(6):
        value = rhs[step]
        for before in range(step):
            value = value - lower[step][before] * forward[before]
        forward.append(value * inverse[step])
    answer = [None] * 6
    for step in range(5, -1, -1):
        value = forward[step]
        for after in range(step + 1, 6):
            value = value - lower[after][step] * answer[after]
        answer[step] = value * inverse[step]
    return answer


UNKNOWNS = [("x", q) for q in range(28)] + [("y", q) for q in range(24, 28)] + [("y", q) for q in range(24)]
SIZE = 2 * POLY
BLOCKS = SIZE // 8
PANEL = 4


def solve_kernel(arr_ref, expand_ref, scale_ref, upd_ref, resp_ref, table, wide, mat, rhs, invs):
    sub8 = iota((8, LANES), 0)
    rows128 = iota((LANES, LANES), 0)
    lanes128 = iota((LANES, LANES), 1)

    picks = []
    for copy in range(2):
        column = arr_ref[:, 3 * copy, :][:, MARK : MARK + 1]
        picks.append((column.astype(jnp.int32) == lanes128 + 1).astype(F32))
    pick = jnp.concatenate(picks, axis=0)
    for block in range(3):
        both = jnp.concatenate([arr_ref[:, block, :], arr_ref[:, 3 + block, :]], axis=0)
        table[pl.ds(block * LANES, LANES), :] = dot(both, pick, ((0,), (0,)))

    sums = [jnp.sum(arr_ref[:, 3 * copy + 2, :], axis=0, keepdims=True) for copy in range(2)]
    turned = jnp.where(rows128 == 0, sums[0], jnp.where(rows128 == 1, sums[1], 0.0)).T
    answer = detector_solve(turned[96:128])

    moments = jnp.concatenate([table[0:96], table[96:192], table[192:288]], axis=1)
    chunk = 224
    for at in range(0, POLY * 32, chunk):
        wide[pl.ds(at, chunk), :] = dot(expand_ref[pl.ds(at, chunk), :], moments, ((1,), (0,)))

    def part(which, q, group):
        return wide[q * 32 + group * 8 : q * 32 + group * 8 + 8, which * LANES : (which + 1) * LANES]

    for col, (kind, q) in enumerate(UNKNOWNS):
        for group in range(col // 8, BLOCKS):
            if kind == "x":
                if group < 3:
                    value = part(0, q, group)
                elif group == 3:
                    value = jnp.where(sub8 < 4, part(0, q, 3), pltpu.roll(part(2, q, 3), 4, 0))
                else:
                    value = part(2, q, group - 4)
            elif group == 3:
                value = jnp.where(sub8 < 4, 0.0, pltpu.roll(part(1, q, 3), 4, 0))
            else:
                value = part(1, q, group - 4)
            if group == col // 8:
                value = value + jnp.where(sub8 == col % 8, EXPOSURE_DAMP, 0.0)
            mat[pl.ds(col * SIZE + group * 8, 8), :] = value
    grad_x = table[ROW_GX : ROW_GX + 32] * scale_ref[...]
    grad_y = table[ROW_GY : ROW_GY + 32] * scale_ref[...]
    rhs[0:24, :] = grad_x[0:24]
    rhs[24:32, :] = jnp.where(sub8 < 4, grad_x[24:32], pltpu.roll(grad_y[24:32], 4, 0))
    rhs[32:56, :] = grad_y[0:24]

    for k0 in range(0, SIZE, PANEL):
        g0 = k0 // 8
        count = BLOCKS - g0

        def update(j, carry):
            base = j * SIZE
            column = [mat[pl.ds(pl.multiple_of(base + g * 8, 8), 8), :] for g in range(g0, BLOCKS)]
            new = []
            for c in range(PANEL):
                factor = mat[pl.ds(base + k0 + c, 1), :]
                for g in range(count):
                    new.append(carry[c * count + g] - column[g] * factor)
            return tuple(new)

        panel = tuple(
            mat[pl.ds((k0 + c) * SIZE + g * 8, 8), :] for c in range(PANEL) for g in range(g0, BLOCKS)
        )
        if k0:
            panel = lax.fori_loop(0, k0, update, panel, unroll=4)
        panel = [list(panel[c * count : (c + 1) * count]) for c in range(PANEL)]
        right = [rhs[pl.ds(g * 8, 8), :] for g in range(g0, BLOCKS)]
        for c in range(PANEL):
            k = k0 + c
            row = k % 8
            inverse = lax.rsqrt(panel[c][0][row : row + 1])
            column = [value * inverse for value in panel[c]]
            for other in range(c + 1, PANEL):
                factor = column[0][k0 % 8 + other : k0 % 8 + other + 1]
                panel[other] = [panel[other][g] - column[g] * factor for g in range(count)]
            forward = right[0][row : row + 1] * inverse
            keep = jnp.where(sub8 <= row, right[0], right[0] - column[0] * forward)
            keep = jnp.where(sub8 == row, forward, keep)
            right = [keep] + [right[g] - column[g] * forward for g in range(1, count)]
            invs[k : k + 1, :] = inverse
            for g in range(count):
                mat[pl.ds(k * SIZE + (g0 + g) * 8, 8), :] = column[g]
        for g in range(count):
            rhs[pl.ds((g0 + g) * 8, 8), :] = right[g]

    solved = [None] * BLOCKS
    for b in range(BLOCKS - 1, -1, -1):
        right = rhs[b * 8 : b * 8 + 8]
        if b < BLOCKS - 1:
            partial = []
            for c in range(8):
                total = None
                for g in range(b + 1, BLOCKS):
                    term = mat[pl.ds((b * 8 + c) * SIZE + g * 8, 8), :] * solved[g]
                    total = term if total is None else total + term
                partial.append(total)
            right = right - combine(partial, sub8)
        diagonal = transpose8([mat[pl.ds((b * 8 + c) * SIZE + b * 8, 8), :] for c in range(8)], sub8)
        for c in range(7, -1, -1):
            value = right[c : c + 1] * invs[b * 8 + c : b * 8 + c + 1]
            right = jnp.where(sub8 < c, right - diagonal[c] * value, jnp.where(sub8 == c, value, right))
        solved[b] = right
    whole = jnp.concatenate(
        solved[0:3] + [solved[3][0:4]] + solved[4:7] + [solved[3][4:8]], axis=0
    )
    upd_ref[...] = whole

    lane1 = iota((1, LANES), 1)
    first = [jnp.where(lane1 == 0, value, 0.0) for value in answer]
    second = [jnp.where(lane1 == 1, value, 0.0) for value in answer]
    zeros = jnp.zeros((SIZE, LANES), F32)
    zero16 = jnp.zeros((16, LANES), F32)
    gap = [jnp.zeros((2, LANES), F32)]
    left = jnp.concatenate(picks + [(lanes128 < 2).astype(F32)], axis=1)
    right = jnp.concatenate(
        [
            jnp.concatenate([whole, zeros, zero16], axis=0),
            jnp.concatenate([zeros, whole, zero16], axis=0),
            jnp.concatenate([zeros, zeros] + first + gap + second + gap, axis=0),
        ],
        axis=1,
    )
    resp_ref[...] = dot(left, right, ((1,), (1,)))


def star_kernel(uv_ref, off_ref, diag_ref, corr_ref, count_ref, uvt_ref, where_ref, scale_ref, resp_ref,
                star_ref, det_ref, coeff, model):
    tiles = corr_ref.shape[0]
    rows128 = iota((LANES, LANES), 0)
    for c in range(2):
        count = (NCCD + 1 - c) // 2
        det_ref[pl.ds(c, count, stride=2), :] = resp_ref[0:count, 112 + 8 * c : 118 + 8 * c]
    turned = resp_ref[...].T
    dest = where_ref[0:1]
    copy_at = where_ref[1:2]
    ccd = where_ref[2:3]
    picks = [((rows128 == dest) & (copy_at == c)).astype(F32) for c in range(2)]
    picks += [(rows128 * 2 + c == ccd).astype(F32) for c in range(2)]
    exposure = dot(turned[0:56], picks[0], ((1,), (0,))) + dot(turned[56:112], picks[1], ((1,), (0,)))
    detector = dot(turned[112:120], picks[2], ((1,), (0,))) + dot(turned[120:128], picks[3], ((1,), (0,)))
    scale = scale_ref[...]
    coeff[0:28, :] = exposure[0:28] * scale[0:28]
    coeff[32:60, :] = exposure[28:56] * scale[0:28]
    for axis in range(2):
        for m, term in enumerate(((0, 0), (1, 0), (0, 1))):
            row = 32 * axis + TERM_INDEX[term]
            coeff[row : row + 1, :] = coeff[row : row + 1, :] + detector[3 * axis + m : 3 * axis + m + 1]

    def evaluate(g, carry):
        at = pl.ds(pl.multiple_of(g * 8, 8), 8)
        in_u = legendre(uvt_ref[0, at, :], ORDER + 1)
        in_v = legendre(uvt_ref[1, at, :], ORDER + 1)
        for axis in range(2):
            total = None
            for i in range(ORDER + 1):
                inner = None
                for j in range(ORDER - i + 1):
                    row = 32 * axis + TERM_INDEX[(i, j)]
                    term = coeff[row : row + 1, :]
                    if j:
                        term = term * in_v[j]
                    inner = term if inner is None else inner + term
                if i:
                    inner = inner * in_u[i]
                total = inner if total is None else total + inner
            model[axis, at, :] = total
        return carry

    lax.fori_loop(0, LANES // 8, evaluate, 0, unroll=2)
    model_x = model[0].T
    model_y = model[1].T
    weights, resid, inverse = star_terms(uv_ref, off_ref, diag_ref, corr_ref, count_ref)
    grad_x = None
    for visit in range(VISITS):
        w_xx, w_yy, w_xy = weights[visit]
        left_x = resid[visit][0] - model_x[visit * tiles : (visit + 1) * tiles]
        left_y = resid[visit][1] - model_y[visit * tiles : (visit + 1) * tiles]
        part_x = w_xx * left_x + w_xy * left_y
        part_y = w_xy * left_x + w_yy * left_y
        grad_x = part_x if grad_x is None else grad_x + part_x
        grad_y = part_y if visit == 0 else grad_y + part_y
    out_x, out_y = apply_inverse(inverse, grad_x, grad_y)
    star_ref[:, 0, :] = out_x
    star_ref[:, 1, :] = out_y


def vmem(count):
    return [pl.BlockSpec(memory_space=pltpu.VMEM)] * count


def shards(focal_uv, offsets, w_diag, w_corr, star_count, exposure_ids, ccd_ids, exp_slot):
    tiles = offsets.shape[0]
    flat = (tiles * VISITS * 2, LANES)
    stars = (
        focal_uv.reshape(flat),
        offsets.reshape(flat),
        w_diag.reshape(flat),
        w_corr,
        star_count.reshape(1, tiles),
    )
    shape = jax.ShapeDtypeStruct
    outgoing, turned, where = pl.pallas_call(
        moments_kernel,
        out_shape=(
            shape((LANES, 6, LANES), F32),
            shape((2, LANES, LANES), F32),
            shape((8, LANES), jnp.int32),
        ),
        in_specs=vmem(8),
        out_specs=tuple(vmem(3)),
        scratch_shapes=[
            pltpu.VMEM((7, LANES, LANES), F32),
            pltpu.VMEM((DEG2 + 1, LANES, LANES), F32),
            pltpu.VMEM((DEG2 + 1, LANES, LANES), F32),
            pltpu.VMEM((ROW_DET * 8, LANES), F32),
            pltpu.VMEM((ROW_DET, LANES), F32),
        ],
        name="moments",
    )(*stars, exposure_ids, ccd_ids, exp_slot.reshape(LANES, LANES))
    arrived = lax.all_to_all(outgoing, ("field", "shard"), 0, 0, tiled=True)
    scale = jnp.asarray(scale_rows())
    update, answers = pl.pallas_call(
        solve_kernel,
        out_shape=(shape((SIZE, LANES), F32), shape((LANES, LANES), F32)),
        in_specs=vmem(3),
        out_specs=tuple(vmem(2)),
        scratch_shapes=[
            pltpu.VMEM((ROWS, LANES), F32),
            pltpu.VMEM((POLY * 32, 3 * LANES), F32),
            pltpu.VMEM((SIZE * SIZE, LANES), F32),
            pltpu.VMEM((SIZE, LANES), F32),
            pltpu.VMEM((SIZE, LANES), F32),
        ],
        name="solve",
    )(arrived, jnp.asarray(expansion()), scale)
    replies = lax.all_to_all(answers.reshape(LANES, 1, LANES), ("field", "shard"), 0, 0, tiled=True)
    star_update, ccd_update = pl.pallas_call(
        star_kernel,
        out_shape=(shape((tiles, 2, LANES), F32), shape((NCCD, 6), F32)),
        in_specs=vmem(9),
        out_specs=tuple(vmem(2)),
        scratch_shapes=[pltpu.VMEM((64, LANES), F32), pltpu.VMEM((2, LANES, LANES), F32)],
        name="stars",
    )(*stars, turned, where, scale, replies.reshape(LANES, LANES))
    return star_update, update, ccd_update


def solution(mesh):
    both = ("field", "shard")
    in_specs = (
        P(both, None, None, None),
        P(both, None, None, None),
        P(both, None, None, None),
        P(both, None, None),
        P(both),
        P(both, None),
        P(both, None),
        P(),
    )
    out_specs = (P(both, None, None), P(None, both), P())
    return jax.shard_map(shards, mesh=mesh, in_specs=in_specs, out_specs=out_specs, check_vma=False)
```

time: 806 us -> 62.3 us (0.08); the launches traced: 791 us -> 61.9 us
  other arithmetic: 458 us -> 0 us
  local copies, waits for them, and re-layouts: 117 us -> 5.05 us
  waiting for transfers between devices: 87.4 us -> 0 us
  matrix products: 30.4 us -> 0 us
  blocking collectives: 67.1 us -> 40.2 us
  between operations: 20.7 us -> 0.64 us
  Pallas kernels: 0 us -> 16 us
  starting transfers between devices: 10.4 us -> 0 us
    sub x176 -> x0, other arithmetic: 377 us -> none  [the longest x60 324 us: batched_cholesky_solve(): work = work - column[:, None, :] * column[None, :, :]]
    psum x1 -> x0, blocking collectives: 67.1 us -> none  [shards(): ccd_table = lax.psum(ccd_local, ('field', 'shard'))]
    all_gather x1 -> x0, waiting for transfers between devices: 58.1 us -> none  [shards(): lax.all_gather(exposure_update, ('field', 'shard'), axis=1, tiled=True)]
    all_to_all x0 -> x2, blocking collectives: none -> 40.2 us  [the longest x1 25.1 us: shards(): arrived = lax.all_to_all(outgoing, ('field', 'shard'), 0, 0, tiled=True)]
    unnamed x494 -> x6, local copies, waits for them, and re-layouts: 44.7 us -> 5.05 us
    select_n x122 -> x0, other arithmetic: 36.9 us -> none  [the longest x118 35.6 us: batched_cholesky_solve(): column = jnp.where((rows_idx >= step)[:, None], column, jnp.float32(0.0))]
    dot_general x14 -> x0, matrix products: 30.4 us -> none  [the longest x6 17.7 us: outer(): jnp.einsum('...ps,...qs->...pq', basis * scale[..., None, :], basis, prec...]
    reduce_scatter x1 -> x0, waiting for transfers between devices: 29.3 us -> none  [shards(): summed = lax.psum_scatter(table, 'field', scatter_dimension=0, tiled=True)]
  transfers between devices with their start and end apart: 3 -> 0, of which waited for: 2 -> 0; matrix products, arithmetic and copies ran while one was open for 5% -> 0% of each run, Pallas kernels for 0% -> 0%
where the time goes in v1:
time: 62.3 us; the launch traced here: 61.9 us
  blocking collectives  40.2 us (65%)
  Pallas kernels  16 us (26%)
  local copies, waits for them, and re-layouts  5.05 us (8%)
  between operations  0.64 us (1%)
    all_to_all x1, blocking collectives, shards(): arrived = lax.all_to_all(outgoing, ('field', 'shard'), 0, 0, tiled=True)  25.1 us
    all_to_all x1, blocking collectives, shards(): lax.all_to_all(answers.reshape(LANES, 1, LANES), ('field', 'shard'), 0, 0...  15.1 us
    pallas_call x1, Pallas kernels, shards(): pl.pallas_call(moments_kernel, out_shape=(shape((LANES, 6, LANES), F32),...  6.69 us
    pallas_call x1, Pallas kernels, shards(): pl.pallas_call(solve_kernel, out_shape=(shape((SIZE, LANES), F32), shape(...  6.65 us
    unnamed x6, local copies, waits for them, and re-layouts  5.05 us
    pallas_call x1, Pallas kernels, shards(): pl.pallas_call(star_kernel, out_shape=(shape((tiles, 2, LANES), F32), sha...  2.64 us

profile of v1, /device:TPU:1, one launch (start us, length us, event | category | flops | bytes accessed | tf_op | source)
XLA Modules:
  0.0 61.9 jit_solution(1058590060583028768)
XLA Ops:
  0.6 0.0 copy-start
  0.6 1.4 %copy.19.ids_ref = s32[16,6]{1,0:T(8,128)} copy(s32[16,6]{0,1:T(8,128)} %param.15) | data formatting | bytes 768 | tf_op args[5]
  2.0 0.0 copy-done
  2.0 0.7 %copy.20.ccd_ref = s32[16,6]{1,0:T(8,128)} copy(s32[16,6]{0,1:T(8,128)S(1)} %copy-done) | data formatting | bytes 768 | tf_op args[6]
  2.7 1.4 %copy.22.corr_ref = f32[16,6,128]{2,1,0:T(8,128)} copy(f32[16,6,128]{2,0,1:T(8,128)} %param.13) | data formatting | bytes 98304 | tf_op args[3]
  4.1 6.7 %moments.1 = (f32[128,6,128]{2,1,0:T(8,128)}, f32[2,128,128]{2,1,0:T(8,128)}, s32[8,128]{1,0:T(8,128)}) custom-call(f32[192,128]{1,0:T(8,128)} %bitcast.9, f32[192,128]{1,0:T(8,128)} %bitcast.11, f32[192,128]{1,0:T(8,128)} %bitcast.13, f32[16,6,128]{2,1,0:T(8,128)} %copy.22.corr_ref, s32[1,16]{1,0:T(1,128)} %bitcast.18, s32[16,6]{1,0:T(8,128)} %copy.19.ids_ref, ...), custom_call_target="tpu_custom_call" | custom-call | tf_op jit(solution)/shard_map/moments/pallas_call | solution.py:525
  10.8 25.1 %all_to_all.10.arr_ref = f32[128,6,128]{2,1,0:T(8,128)} all-to-all(f32[128,6,128]{2,1,0:T(8,128)} %get-tuple-element.12), channel_id=1, replica_groups=mesh['field'=4,'shard'=32] {'field','shard'}, dimensions={0} | all-to-all | bytes 786432 | tf_op jit(solution)/shard_map/all_to_all | solution.py:543
  35.9 6.6 %solve.1 = (f32[56,128]{1,0:T(8,128)}, f32[128,128]{1,0:T(8,128)}) custom-call(f32[128,6,128]{2,1,0:T(8,128)} %all_to_all.10.arr_ref, f32[896,96]{1,0:T(8,128)} %constant.5.clone.expand_ref, f32[32,128]{1,0:T(8,128)} %constant.4.clone.scale_ref), custom_call_target="tpu_custom_call" | custom-call | tf_op jit(solution)/shard_map/solve/pallas_call | solution.py:545
  42.5 15.1 %all_to_all.11 = f32[128,1,128]{2,1,0:T(1,128)} all-to-all(f32[128,1,128]{2,1,0:T(1,128)} %bitcast.16), channel_id=1, replica_groups=mesh['field'=4,'shard'=32] {'field','shard'}, dimensions={0} | all-to-all | bytes 131072 | tf_op jit(solution)/shard_map/all_to_all | solution.py:559
  57.7 2.6 %stars.1 = (f32[16,2,128]{2,1,0:T(2,128)}, f32[189,6]{1,0:T(8,128)}) custom-call(f32[192,128]{1,0:T(8,128)} %bitcast.10, f32[192,128]{1,0:T(8,128)} %bitcast.12, f32[192,128]{1,0:T(8,128)} %bitcast.14, f32[16,6,128]{2,1,0:T(8,128)} %copy.22.corr_ref, s32[1,16]{1,0:T(1,128)} %bitcast.19, f32[2,128,128]{2,1,0:T(8,128)} %get-tuple-element.10.uvt_ref, ...), custom_call_target="tpu_custom_call" | custom-call | tf_op jit(solution)/shard_map/stars/pallas_call | solution.py:560
  60.3 1.6 %copy.23 = f32[189,6]{0,1:T(8,128)} copy(f32[189,6]{1,0:T(8,128)} %get-tuple-element.22) | data formatting | bytes 9072
Async XLA Ops:
  0.6 1.4 %copy-start = (s32[16,6]{0,1:T(8,128)S(1)}, s32[16,6]{0,1:T(8,128)}, u32[]{:S(2)}) copy-start(s32[16,6]{0,1:T(8,128)} %param.16) | copy-start | bytes 1156

commit v2 on v1

--- a/solution.py
+++ b/solution.py
@@ -62,6 +62,10 @@
     return lax.dot_general(a, b, (dims, ((), ())), precision=HIGH, preferred_element_type=F32)
 
 
+def rows_of(part):
+    return pl.ds(part, LANES, stride=6)
+
+
 def iota(shape, axis):
     return lax.broadcasted_iota(jnp.int32, shape, axis)
 
@@ -74,10 +78,10 @@
     return values
 
 
-def star_terms(uv_ref, off_ref, diag_ref, corr_ref, count_ref):
-    tiles = corr_ref.shape[0]
+def star_terms(off_ref, diag_ref, corr_ref, counts):
+    tiles = corr_ref.shape[1]
     lanes = iota((tiles, LANES), 1)
-    counts = jnp.broadcast_to(count_ref[...].astype(F32), (tiles, tiles))
+    counts = jnp.broadcast_to(counts.astype(F32), (tiles, tiles))
     square = (iota((tiles, tiles), 0) == iota((tiles, tiles), 1)).astype(F32)
     column = jnp.sum(counts * square, axis=1, keepdims=True)
     present = (lanes.astype(F32) < column).astype(F32)
@@ -90,7 +94,7 @@
     for visit in range(VISITS):
         d0 = rows(diag_ref, visit, 0)
         d1 = rows(diag_ref, visit, 1)
-        weights.append((d0 * present, d1 * present, corr_ref[:, visit, :] * jnp.sqrt(d0 * d1) * present))
+        weights.append((d0 * present, d1 * present, corr_ref[visit] * jnp.sqrt(d0 * d1) * present))
         resid.append((rows(off_ref, visit, 0), rows(off_ref, visit, 1)))
     hess_xx = sum(w[0] for w in weights) + STAR_DAMP
     hess_yy = sum(w[1] for w in weights) + STAR_DAMP
@@ -133,21 +137,34 @@
     return values
 
 
-def moments_kernel(uv_ref, off_ref, diag_ref, corr_ref, count_ref, ids_ref, ccd_ref, slot_ref,
-                   out_ref, uvt_ref, where_ref, chan, pu, pv, acc, mom):
-    tiles = corr_ref.shape[0]
+def moments_kernel(*refs):
+    sources, out_refs, buffers, (sems, *scratch) = refs[:8], refs[8:11], refs[11:19], refs[19:]
+    copies = [
+        pltpu.make_async_copy(source, buffer, sems.at[at])
+        for at, (source, buffer) in enumerate(zip(sources, buffers))
+    ]
+    for copy in copies:
+        copy.start()
+    for copy in copies:
+        copy.wait()
+    moments_body(*buffers, *out_refs, *scratch)
+
+
+def moments_body(uv_ref, off_ref, diag_ref, corr_ref, count_ref, ids_ref, ccd_ref, slot_ref,
+                 out_ref, uvt_ref, where_ref, chan, pu, pv, acc, mom):
+    tiles = corr_ref.shape[1]
     visits_all = tiles * VISITS
     sub8 = iota((8, LANES), 0)
 
-    lane16 = iota((tiles, LANES), 1)
     pad = jnp.zeros((LANES - visits_all, LANES), F32)
-    ids = [
-        jnp.where(lane16 < 64, ids_ref[:, k : k + 1], ccd_ref[:, k : k + 1]).astype(F32)
-        for k in range(VISITS)
-    ]
-    turned = jnp.concatenate(ids + [pad], axis=0).T
-    ident = turned[0:1].astype(jnp.int32)
-    ccd = turned[64:65].astype(jnp.int32)
+    mine = iota((VISITS, LANES), 1) // tiles == iota((VISITS, LANES), 0)
+
+    def along_lanes(ref):
+        spread = jnp.concatenate([ref[...]] * (LANES // tiles), axis=1)
+        return jnp.sum(jnp.where(mine, spread, 0), axis=0, keepdims=True)
+
+    ident = along_lanes(ids_ref)
+    ccd = along_lanes(ccd_ref)
     rows128 = iota((LANES, LANES), 0)
     lanes128 = iota((LANES, LANES), 1)
     valid = iota((1, LANES), 1) < visits_all
@@ -155,14 +172,17 @@
     position = jnp.sum(jnp.where(rows128 == ident % LANES, picked, 0.0), axis=0, keepdims=True)
     position = (position + 0.5).astype(jnp.int32)
     dest = jnp.where(valid, position // LANES, -1)
-    ccd = jnp.where(valid, ccd, -2)
+    ccd = jnp.where(valid, ccd, -1)
     dest_t = jnp.broadcast_to(dest.astype(F32), (LANES, LANES)).T.astype(jnp.int32)
     same = (dest_t == dest) & (rows128 < lanes128)
     copy_at = jnp.sum(same.astype(F32), axis=0, keepdims=True).astype(jnp.int32)
     mark = (position % LANES + 1).astype(F32)
-    where_ref[...] = jnp.where(sub8 == 0, dest, jnp.where(sub8 == 1, copy_at, ccd))
-
-    weights, resid, inverse = star_terms(uv_ref, off_ref, diag_ref, corr_ref, count_ref)
+    counts = jnp.concatenate([count_ref[...]] * (LANES // tiles), axis=1)
+    where_ref[...] = jnp.where(
+        sub8 == 0, dest, jnp.where(sub8 == 1, copy_at, jnp.where(sub8 == 2, ccd, counts))
+    )
+
+    weights, resid, inverse = star_terms(off_ref, diag_ref, corr_ref, count_ref[...])
     grad_x = sum(w[0] * r[0] + w[2] * r[1] for w, r in zip(weights, resid))
     grad_y = sum(w[2] * r[0] + w[1] * r[1] for w, r in zip(weights, resid))
     shift_x, shift_y = apply_inverse(inverse, grad_x, grad_y)
@@ -261,10 +281,10 @@
     )
     for copy in range(2):
         place = ((rows128 == dest) & (copy_at == copy)).astype(F32)
-        place_det = (rows128 * 2 + copy == ccd).astype(F32)
-        out_ref[:, 3 * copy, :] = dot(place, mom[0:128], ((1,), (1,)))
-        out_ref[:, 3 * copy + 1, :] = dot(place, mom[128:256], ((1,), (1,)))
-        out_ref[:, 3 * copy + 2, :] = dot(
+        place_det = (rows128 + LANES * copy == ccd).astype(F32)
+        out_ref[rows_of(3 * copy), :] = dot(place, mom[0:128], ((1,), (1,)))
+        out_ref[rows_of(3 * copy + 1), :] = dot(place, mom[128:256], ((1,), (1,)))
+        out_ref[rows_of(3 * copy + 2), :] = dot(
             jnp.concatenate([place, place_det], axis=1), last, ((1,), (1,))
         )
 
@@ -326,14 +346,14 @@
 
     picks = []
     for copy in range(2):
-        column = arr_ref[:, 3 * copy, :][:, MARK : MARK + 1]
+        column = arr_ref[rows_of(3 * copy), :][:, MARK : MARK + 1]
         picks.append((column.astype(jnp.int32) == lanes128 + 1).astype(F32))
     pick = jnp.concatenate(picks, axis=0)
     for block in range(3):
-        both = jnp.concatenate([arr_ref[:, block, :], arr_ref[:, 3 + block, :]], axis=0)
+        both = jnp.concatenate([arr_ref[rows_of(block), :], arr_ref[rows_of(3 + block), :]], axis=0)
         table[pl.ds(block * LANES, LANES), :] = dot(both, pick, ((0,), (0,)))
 
-    sums = [jnp.sum(arr_ref[:, 3 * copy + 2, :], axis=0, keepdims=True) for copy in range(2)]
+    sums = [jnp.sum(arr_ref[rows_of(3 * copy + 2), :], axis=0, keepdims=True) for copy in range(2)]
     turned = jnp.where(rows128 == 0, sums[0], jnp.where(rows128 == 1, sums[1], 0.0)).T
     answer = detector_solve(turned[96:128])
 
@@ -446,19 +466,18 @@
     resp_ref[...] = dot(left, right, ((1,), (1,)))
 
 
-def star_kernel(uv_ref, off_ref, diag_ref, corr_ref, count_ref, uvt_ref, where_ref, scale_ref, resp_ref,
+def star_kernel(off_ref, diag_ref, corr_ref, uvt_ref, where_ref, scale_ref, resp_ref,
                 star_ref, det_ref, coeff, model):
-    tiles = corr_ref.shape[0]
+    tiles = corr_ref.shape[1]
     rows128 = iota((LANES, LANES), 0)
-    for c in range(2):
-        count = (NCCD + 1 - c) // 2
-        det_ref[pl.ds(c, count, stride=2), :] = resp_ref[0:count, 112 + 8 * c : 118 + 8 * c]
     turned = resp_ref[...].T
+    det_ref[:, 0:LANES] = turned[112:118]
+    det_ref[:, LANES:NCCD] = turned[120:126, 0 : NCCD - LANES]
     dest = where_ref[0:1]
     copy_at = where_ref[1:2]
     ccd = where_ref[2:3]
     picks = [((rows128 == dest) & (copy_at == c)).astype(F32) for c in range(2)]
-    picks += [(rows128 * 2 + c == ccd).astype(F32) for c in range(2)]
+    picks += [(rows128 + LANES * c == ccd).astype(F32) for c in range(2)]
     exposure = dot(turned[0:56], picks[0], ((1,), (0,))) + dot(turned[56:112], picks[1], ((1,), (0,)))
     detector = dot(turned[112:120], picks[2], ((1,), (0,))) + dot(turned[120:128], picks[3], ((1,), (0,)))
     scale = scale_ref[...]
@@ -492,7 +511,7 @@
     lax.fori_loop(0, LANES // 8, evaluate, 0, unroll=2)
     model_x = model[0].T
     model_y = model[1].T
-    weights, resid, inverse = star_terms(uv_ref, off_ref, diag_ref, corr_ref, count_ref)
+    weights, resid, inverse = star_terms(off_ref, diag_ref, corr_ref, where_ref[3:4, 0:tiles])
     grad_x = None
     for visit in range(VISITS):
         w_xx, w_yy, w_xy = weights[visit]
@@ -514,33 +533,40 @@
 def shards(focal_uv, offsets, w_diag, w_corr, star_count, exposure_ids, ccd_ids, exp_slot):
     tiles = offsets.shape[0]
     flat = (tiles * VISITS * 2, LANES)
-    stars = (
+    inputs = (
         focal_uv.reshape(flat),
         offsets.reshape(flat),
         w_diag.reshape(flat),
-        w_corr,
+        jnp.transpose(w_corr, (1, 0, 2)),
         star_count.reshape(1, tiles),
+        exposure_ids.T,
+        ccd_ids.T,
+        exp_slot.reshape(LANES, LANES),
     )
     shape = jax.ShapeDtypeStruct
     outgoing, turned, where = pl.pallas_call(
         moments_kernel,
         out_shape=(
-            shape((LANES, 6, LANES), F32),
+            shape((6 * LANES, LANES), F32),
             shape((2, LANES, LANES), F32),
             shape((8, LANES), jnp.int32),
         ),
-        in_specs=vmem(8),
+        in_specs=[pl.BlockSpec(memory_space=pltpu.HBM)] * 8,
         out_specs=tuple(vmem(3)),
-        scratch_shapes=[
+        scratch_shapes=[pltpu.VMEM(array.shape, array.dtype) for array in inputs]
+        + [
+            pltpu.SemaphoreType.DMA((8,)),
             pltpu.VMEM((7, LANES, LANES), F32),
             pltpu.VMEM((DEG2 + 1, LANES, LANES), F32),
             pltpu.VMEM((DEG2 + 1, LANES, LANES), F32),
             pltpu.VMEM((ROW_DET * 8, LANES), F32),
             pltpu.VMEM((ROW_DET, LANES), F32),
         ],
+        compiler_params=pltpu.CompilerParams(vmem_limit_bytes=12 << 20),
         name="moments",
-    )(*stars, exposure_ids, ccd_ids, exp_slot.reshape(LANES, LANES))
-    arrived = lax.all_to_all(outgoing, ("field", "shard"), 0, 0, tiled=True)
+    )(*(pltpu.with_memory_space_constraint(array, pltpu.HBM) for array in inputs))
+    arrived = lax.all_to_all(outgoing.reshape(LANES, 1, 6 * LANES), ("field", "shard"), 0, 0, tiled=True)
+    arrived = arrived.reshape(6 * LANES, LANES)
     scale = jnp.asarray(scale_rows())
     update, answers = pl.pallas_call(
         solve_kernel,
@@ -554,18 +580,20 @@
             pltpu.VMEM((SIZE, LANES), F32),
             pltpu.VMEM((SIZE, LANES), F32),
         ],
+        compiler_params=pltpu.CompilerParams(vmem_limit_bytes=12 << 20),
         name="solve",
     )(arrived, jnp.asarray(expansion()), scale)
     replies = lax.all_to_all(answers.reshape(LANES, 1, LANES), ("field", "shard"), 0, 0, tiled=True)
     star_update, ccd_update = pl.pallas_call(
         star_kernel,
-        out_shape=(shape((tiles, 2, LANES), F32), shape((NCCD, 6), F32)),
-        in_specs=vmem(9),
+        out_shape=(shape((tiles, 2, LANES), F32), shape((6, NCCD), F32)),
+        in_specs=vmem(7),
         out_specs=tuple(vmem(2)),
         scratch_shapes=[pltpu.VMEM((64, LANES), F32), pltpu.VMEM((2, LANES, LANES), F32)],
+        compiler_params=pltpu.CompilerParams(vmem_limit_bytes=12 << 20),
         name="stars",
-    )(*stars, turned, where, scale, replies.reshape(LANES, LANES))
-    return star_update, update, ccd_update
+    )(*inputs[1:4], turned, where, scale, replies.reshape(LANES, LANES))
+    return star_update, update, ccd_update.T
 
 
 def solution(mesh):

time: 62.3 us -> 50.5 us (0.81)
  local copies, waits for them, and re-layouts: 5.05 us -> 0.02 us
  Pallas kernels: 16 us -> 12.1 us
  blocking collectives: 40.2 us -> 37.5 us
    unnamed x6 -> x10, local copies, waits for them, and re-layouts: 5.05 us -> 0.02 us
    pallas_call x1, Pallas kernels: 6.65 us -> 4.77 us  [shards(): pl.pallas_call(solve_kernel, out_shape=(shape((SIZE, LANES), F32), shape(...]
    all_to_all x1, blocking collectives: 25.1 us -> 23.4 us  [shards(): lax.all_to_all(outgoing.reshape(LANES, 1, 6 * LANES), ('field', 'shard'),...]
    pallas_call x1, Pallas kernels: 2.64 us -> 1.53 us  [shards(): pl.pallas_call(star_kernel, out_shape=(shape((tiles, 2, LANES), F32), sha...]
    all_to_all x1, blocking collectives: 15.1 us -> 14.1 us  [shards(): lax.all_to_all(answers.reshape(LANES, 1, LANES), ('field', 'shard'), 0, 0...]
    pallas_call x1, Pallas kernels: 6.69 us -> 5.8 us  [shards(): pl.pallas_call(moments_kernel, out_shape=(shape((6 * LANES, LANES), F32),...]
where the time goes in v2:
time: 50.5 us; the launch traced here: 50.3 us
  blocking collectives  37.5 us (74%)
  Pallas kernels  12.1 us (24%)
  between operations  0.67 us (1%)
    all_to_all x1, blocking collectives, shards(): lax.all_to_all(outgoing.reshape(LANES, 1, 6 * LANES), ('field', 'shard'),...  23.4 us
    all_to_all x1, blocking collectives, shards(): lax.all_to_all(answers.reshape(LANES, 1, LANES), ('field', 'shard'), 0, 0...  14.1 us
    pallas_call x1, Pallas kernels, shards(): pl.pallas_call(moments_kernel, out_shape=(shape((6 * LANES, LANES), F32),...  5.8 us
    pallas_call x1, Pallas kernels, shards(): pl.pallas_call(solve_kernel, out_shape=(shape((SIZE, LANES), F32), shape(...  4.77 us
    pallas_call x1, Pallas kernels, shards(): pl.pallas_call(star_kernel, out_shape=(shape((tiles, 2, LANES), F32), sha...  1.53 us

profile of v2, /device:TPU:1, one launch (start us, length us, event | category | flops | bytes accessed | tf_op | source)
XLA Modules:
  0.0 50.3 jit_solution(13690571538819225439)
XLA Ops:
  0.6 5.8 %moments.1 = (f32[768,128]{1,0:T(8,128)S(1)}, f32[2,128,128]{2,1,0:T(8,128)S(1)}, s32[8,128]{1,0:T(8,128)S(1)}) custom-call(f32[192,128]{1,0:T(8,128)} %bitcast.25, f32[192,128]{1,0:T(8,128)} %bitcast.17, f32[192,128]{1,0:T(8,128)} %bitcast.19, f32[6,16,128]{2,1,0:T(8,128)} %bitcast.22, s32[1,16]{1,0:T(1,128)} %bitcast.29, s32[6,16]{1,0:T(8,128)} %bitcast.27, ...), custom_call_target="tpu_custom_call" | custom-call | tf_op jit(solution)/shard_map/moments/pallas_call | solution.py:547
  6.4 0.0 copy-start
  6.5 0.0 copy-start.4
  6.5 23.4 %all_to_all.10 = f32[128,1,768]{2,1,0:T(1,128)S(1)} all-to-all(f32[128,1,768]{2,1,0:T(1,128)S(1)} %bitcast.16), channel_id=1, replica_groups=mesh['field'=4,'shard'=32] {'field','shard'}, dimensions={0} | all-to-all | bytes 786432 | tf_op jit(solution)/shard_map/all_to_all | solution.py:568
  29.8 0.0 copy-done
  29.8 0.0 copy-done.4
  29.8 0.0 copy-start.2
  29.8 0.0 copy-start.3
  29.8 4.8 %solve.1 = (f32[56,128]{1,0:T(8,128)}, f32[128,128]{1,0:T(8,128)S(1)}) custom-call(f32[768,128]{1,0:T(8,128)S(1)} %bitcast.15, f32[896,96]{1,0:T(8,128)S(1)} %copy-done, f32[32,128]{1,0:T(8,128)S(1)} %copy-done.4), custom_call_target="tpu_custom_call" | custom-call | tf_op jit(solution)/shard_map/solve/pallas_call | solution.py:571
  34.6 0.0 copy-start.1
  34.6 14.1 %all_to_all.11 = f32[128,1,128]{2,1,0:T(1,128)S(1)} all-to-all(f32[128,1,128]{2,1,0:T(1,128)S(1)} %bitcast.24), channel_id=1, replica_groups=mesh['field'=4,'shard'=32] {'field','shard'}, dimensions={0} | all-to-all | bytes 131072 | tf_op jit(solution)/shard_map/all_to_all | solution.py:586
  48.8 0.0 copy-done.2
  48.8 0.0 copy-done.3
  48.8 0.0 copy-done.1
  48.8 1.5 %stars.1 = (f32[16,2,128]{2,1,0:T(2,128)}, f32[6,189]{1,0:T(8,128)}) custom-call(f32[192,128]{1,0:T(8,128)S(1)} %bitcast.18, f32[192,128]{1,0:T(8,128)S(1)} %bitcast.20, f32[6,16,128]{2,1,0:T(8,128)S(1)} %bitcast.23, f32[2,128,128]{2,1,0:T(8,128)S(1)} %get-tuple-element.10.uvt_ref, s32[8,128]{1,0:T(8,128)S(1)} %get-tuple-element.11.where_ref, ...), custom_call_target="tpu_custom_call" | custom-call | tf_op jit(solution)/shard_map/stars/pallas_call | solution.py:587
Async XLA Ops:
  6.4 23.4 %copy-start = (f32[896,96]{1,0:T(8,128)S(1)}, f32[896,96]{1,0:T(8,128)}, u32[]{:S(2)}) copy-start(f32[896,96]{1,0:T(8,128)} %constant.5.clone.expand_ref) | copy-start | bytes 1032196
  6.5 23.4 %copy-start.4 = (f32[32,128]{1,0:T(8,128)S(1)}, f32[32,128]{1,0:T(8,128)}, u32[]{:S(2)}) copy-start(f32[32,128]{1,0:T(8,128)} %constant.4.clone.scale_ref) | copy-start | bytes 49156
  29.8 18.9 %copy-start.2 = (f32[16,6,2,128]{3,2,1,0:T(2,128)S(1)}, f32[16,6,2,128]{3,2,1,0:T(2,128)}, u32[]{:S(2)}) copy-start(f32[16,6,2,128]{3,2,1,0:T(2,128)} %param.12) | copy-start | bytes 294916
  29.8 18.9 %copy-start.3 = (f32[16,6,128]{2,0,1:T(8,128)S(1)}, f32[16,6,128]{2,0,1:T(8,128)}, u32[]{:S(2)}) copy-start(f32[16,6,128]{2,0,1:T(8,128)} %param.13) | copy-start | bytes 147460
  34.6 14.1 %copy-start.1 = (f32[16,6,2,128]{3,2,1,0:T(2,128)S(1)}, f32[16,6,2,128]{3,2,1,0:T(2,128)}, u32[]{:S(2)}) copy-start(f32[16,6,2,128]{3,2,1,0:T(2,128)} %param.11) | copy-start | bytes 294916

commit v3 on v2

--- a/solution.py
+++ b/solution.py
@@ -49,7 +49,14 @@
         for p, (ip, jp) in enumerate(TERMS[:POLY]):
             for at, (a, b) in enumerate(TERMS):
                 matrix[q * 32 + p, at] = SCALE[p] * SCALE[q] * table[ip, iq, a] * table[jp, jq, b]
-    return matrix.astype(np.float32)
+    parts = []
+    rest = matrix
+    for _ in range(3):
+        part = rest.astype(jnp.bfloat16)
+        parts.append(part)
+        rest = rest - part.astype(np.float64)
+    high, middle, low = parts
+    return np.stack([np.concatenate(pair, 1) for pair in ((high, high), (middle, middle), (high, low))])
 
 
 def scale_rows():
@@ -60,6 +67,17 @@
 
 def dot(a, b, dims):
     return lax.dot_general(a, b, (dims, ((), ())), precision=HIGH, preferred_element_type=F32)
+
+
+def split3(value):
+    high = value.astype(jnp.bfloat16)
+    rest = value - high.astype(F32)
+    middle = rest.astype(jnp.bfloat16)
+    return high, middle, (rest - middle.astype(F32)).astype(jnp.bfloat16)
+
+
+def dot16(a, b, dims):
+    return lax.dot_general(a, b, (dims, ((), ())), preferred_element_type=F32)
 
 
 def rows_of(part):
@@ -138,16 +156,18 @@
 
 
 def moments_kernel(*refs):
-    sources, out_refs, buffers, (sems, *scratch) = refs[:8], refs[8:11], refs[11:19], refs[19:]
+    sources, out_refs, buffers, (sems, *scratch) = refs[:10], refs[10:15], refs[15:23], refs[23:]
     copies = [
         pltpu.make_async_copy(source, buffer, sems.at[at])
-        for at, (source, buffer) in enumerate(zip(sources, buffers))
+        for at, (source, buffer) in enumerate(zip(sources, (*buffers, *out_refs[3:])))
     ]
     for copy in copies:
         copy.start()
-    for copy in copies:
+    for copy in copies[:8]:
         copy.wait()
-    moments_body(*buffers, *out_refs, *scratch)
+    moments_body(*buffers, *out_refs[:3], *scratch)
+    for copy in copies[8:]:
+        copy.wait()
 
 
 def moments_body(uv_ref, off_ref, diag_ref, corr_ref, count_ref, ids_ref, ccd_ref, slot_ref,
@@ -214,35 +234,28 @@
 
     groups = LANES // 8
 
-    def tables(g, carry):
-        at = pl.ds(pl.multiple_of(g * 8, 8), 8)
+    for g in range(groups):
+        at = pl.ds(g * 8, 8)
         for ref, source in ((pu, 0), (pv, 1)):
             for degree, value in enumerate(legendre(chan[source, at, :], DEG2 + 1)):
                 if degree:
                     ref[degree, at, :] = value
-        return carry
-
-    lax.fori_loop(0, groups, tables, 0)
 
     def sweep(i, top, first, count, row0, width):
         heights = top - i + 1
-
-        def step(g, carry):
-            at = pl.ds(pl.multiple_of(g * 8, 8), 8)
+        sums = [None] * (heights * count)
+        for g in range(groups):
+            at = pl.ds(g * 8, 8)
             scaled = [chan[first + w, at, :] for w in range(count)]
             if i:
                 factor = pu[i, at, :]
                 scaled = [value * factor for value in scaled]
-            new = []
             for j in range(heights):
                 other = pv[j, at, :] if j else None
                 for w in range(count):
                     term = scaled[w] * other if j else scaled[w]
-                    new.append(carry[j * count + w] + term)
-            return tuple(new)
-
-        start = tuple(jnp.zeros((8, LANES), F32) for _ in range(heights * count))
-        sums = lax.fori_loop(0, groups, step, start, unroll=2)
+                    before = sums[j * count + w]
+                    sums[j * count + w] = term if before is None else before + term
         for j in range(heights):
             for w in range(count):
                 row = row0 + w * width + TERM_INDEX[(i, j)]
@@ -260,32 +273,27 @@
         for row in range(POLY, 32):
             acc[pl.ds((ROW_GX + block * 32 + row) * 8, 8), :] = zero
 
-    def reduce_rows(g, carry):
-        base = pl.multiple_of(g * 64, 64)
-        mom[pl.ds(pl.multiple_of(g * 8, 8), 8), :] = combine(
-            [acc[pl.ds(base + 8 * s, 8), :] for s in range(8)], sub8
-        )
-        return carry
-
-    lax.fori_loop(0, ROW_DET // 8, reduce_rows, 0, unroll=2)
+    for g in range(ROW_DET // 8):
+        mom[pl.ds(g * 8, 8), :] = combine([acc[pl.ds(g * 64 + 8 * s, 8), :] for s in range(8)], sub8)
     mom[88:96, :] = jnp.where(sub8 == 7, mark, mom[88:96, :])
 
-    zeros96 = jnp.zeros((96, LANES), F32)
     pulls = jnp.where(sub8 < 4, mom[ROW_GX : ROW_GX + 8], pltpu.roll(mom[ROW_GY : ROW_GY + 8], 4, 0))
-    last = jnp.concatenate(
-        [
-            jnp.concatenate([mom[256:352], jnp.zeros((32, LANES), F32)], axis=0),
-            jnp.concatenate([zeros96, mom[0:8], mom[96:104], mom[192:200], pulls], axis=0),
-        ],
-        axis=1,
-    )
+    zero32 = jnp.zeros((32, LANES), F32)
+    zero96 = jnp.zeros((96, LANES), F32)
+    first = split3(mom[0:256])
+    third = split3(jnp.concatenate([mom[256:352], zero32], axis=0))
+    fourth = split3(jnp.concatenate([zero96, mom[0:8], mom[96:104], mom[192:200], pulls], axis=0))
+    pair = jnp.concatenate(first[:2], axis=1)
     for copy in range(2):
-        place = ((rows128 == dest) & (copy_at == copy)).astype(F32)
-        place_det = (rows128 + LANES * copy == ccd).astype(F32)
-        out_ref[rows_of(3 * copy), :] = dot(place, mom[0:128], ((1,), (1,)))
-        out_ref[rows_of(3 * copy + 1), :] = dot(place, mom[128:256], ((1,), (1,)))
-        out_ref[rows_of(3 * copy + 2), :] = dot(
-            jnp.concatenate([place, place_det], axis=1), last, ((1,), (1,))
+        place = ((rows128 == dest) & (copy_at == copy)).astype(jnp.bfloat16)
+        place_det = (rows128 + LANES * copy == ccd).astype(jnp.bfloat16)
+        twice = jnp.concatenate([place, place], axis=1)
+        front = dot16(twice, pair, ((1,), (1,))) + dot16(place, first[2], ((1,), (1,)))
+        out_ref[rows_of(3 * copy), :] = front[:, 0:LANES]
+        out_ref[rows_of(3 * copy + 1), :] = front[:, LANES:]
+        both = jnp.concatenate([place, place_det], axis=1)
+        out_ref[rows_of(3 * copy + 2), :] = sum(
+            dot16(both, jnp.concatenate(parts, axis=1), ((1,), (1,))) for parts in zip(third, fourth)
         )
 
 
@@ -347,20 +355,27 @@
     picks = []
     for copy in range(2):
         column = arr_ref[rows_of(3 * copy), :][:, MARK : MARK + 1]
-        picks.append((column.astype(jnp.int32) == lanes128 + 1).astype(F32))
+        picks.append((column.astype(jnp.int32) == lanes128 + 1).astype(jnp.bfloat16))
     pick = jnp.concatenate(picks, axis=0)
     for block in range(3):
         both = jnp.concatenate([arr_ref[rows_of(block), :], arr_ref[rows_of(3 + block), :]], axis=0)
-        table[pl.ds(block * LANES, LANES), :] = dot(both, pick, ((0,), (0,)))
+        table[pl.ds(block * LANES, LANES), :] = sum(
+            dot16(value, pick, ((0,), (0,))) for value in split3(both)
+        )
 
     sums = [jnp.sum(arr_ref[rows_of(3 * copy + 2), :], axis=0, keepdims=True) for copy in range(2)]
     turned = jnp.where(rows128 == 0, sums[0], jnp.where(rows128 == 1, sums[1], 0.0)).T
     answer = detector_solve(turned[96:128])
 
-    moments = jnp.concatenate([table[0:96], table[96:192], table[192:288]], axis=1)
-    chunk = 224
+    high, middle, low = split3(jnp.concatenate([table[0:96], table[96:192], table[192:288]], axis=1))
+    upper = jnp.concatenate([high, middle], axis=0)
+    lower = jnp.concatenate([low, high], axis=0)
+    chunk = 128
     for at in range(0, POLY * 32, chunk):
-        wide[pl.ds(at, chunk), :] = dot(expand_ref[pl.ds(at, chunk), :], moments, ((1,), (0,)))
+        sides = ((0, upper), (1, upper), (2, lower))
+        wide[pl.ds(at, chunk), :] = sum(
+            dot16(expand_ref[side, pl.ds(at, chunk), :], values, ((1,), (0,))) for side, values in sides
+        )
 
     def part(which, q, group):
         return wide[q * 32 + group * 8 : q * 32 + group * 8 + 8, which * LANES : (which + 1) * LANES]
@@ -393,7 +408,7 @@
 
         def update(j, carry):
             base = j * SIZE
-            column = [mat[pl.ds(pl.multiple_of(base + g * 8, 8), 8), :] for g in range(g0, BLOCKS)]
+            column = [mat[pl.ds(base + g * 8, 8), :] for g in range(g0, BLOCKS)]
             new = []
             for c in range(PANEL):
                 factor = mat[pl.ds(base + k0 + c, 1), :]
@@ -404,8 +419,8 @@
         panel = tuple(
             mat[pl.ds((k0 + c) * SIZE + g * 8, 8), :] for c in range(PANEL) for g in range(g0, BLOCKS)
         )
-        if k0:
-            panel = lax.fori_loop(0, k0, update, panel, unroll=4)
+        for j in range(k0):
+            panel = update(j, panel)
         panel = [list(panel[c * count : (c + 1) * count]) for c in range(PANEL)]
         right = [rhs[pl.ds(g * 8, 8), :] for g in range(g0, BLOCKS)]
         for c in range(PANEL):
@@ -454,7 +469,7 @@
     zeros = jnp.zeros((SIZE, LANES), F32)
     zero16 = jnp.zeros((16, LANES), F32)
     gap = [jnp.zeros((2, LANES), F32)]
-    left = jnp.concatenate(picks + [(lanes128 < 2).astype(F32)], axis=1)
+    left = jnp.concatenate(picks + [(lanes128 < 2).astype(jnp.bfloat16)], axis=1)
     right = jnp.concatenate(
         [
             jnp.concatenate([whole, zeros, zero16], axis=0),
@@ -463,7 +478,7 @@
         ],
         axis=1,
     )
-    resp_ref[...] = dot(left, right, ((1,), (1,)))
+    resp_ref[...] = sum(dot16(left, value, ((1,), (1,))) for value in split3(right))
 
 
 def star_kernel(off_ref, diag_ref, corr_ref, uvt_ref, where_ref, scale_ref, resp_ref,
@@ -544,18 +559,20 @@
         exp_slot.reshape(LANES, LANES),
     )
     shape = jax.ShapeDtypeStruct
-    outgoing, turned, where = pl.pallas_call(
+    tables = (jnp.asarray(expansion()), jnp.asarray(scale_rows()))
+    outgoing, turned, where, expand, scale = pl.pallas_call(
         moments_kernel,
         out_shape=(
             shape((6 * LANES, LANES), F32),
             shape((2, LANES, LANES), F32),
             shape((8, LANES), jnp.int32),
+            *(shape(array.shape, array.dtype) for array in tables),
         ),
-        in_specs=[pl.BlockSpec(memory_space=pltpu.HBM)] * 8,
-        out_specs=tuple(vmem(3)),
+        in_specs=[pl.BlockSpec(memory_space=pltpu.HBM)] * 10,
+        out_specs=tuple(vmem(5)),
         scratch_shapes=[pltpu.VMEM(array.shape, array.dtype) for array in inputs]
         + [
-            pltpu.SemaphoreType.DMA((8,)),
+            pltpu.SemaphoreType.DMA((10,)),
             pltpu.VMEM((7, LANES, LANES), F32),
             pltpu.VMEM((DEG2 + 1, LANES, LANES), F32),
             pltpu.VMEM((DEG2 + 1, LANES, LANES), F32),
@@ -564,10 +581,9 @@
         ],
         compiler_params=pltpu.CompilerParams(vmem_limit_bytes=12 << 20),
         name="moments",
-    )(*(pltpu.with_memory_space_constraint(array, pltpu.HBM) for array in inputs))
+    )(*(pltpu.with_memory_space_constraint(array, pltpu.HBM) for array in (*inputs, *tables)))
     arrived = lax.all_to_all(outgoing.reshape(LANES, 1, 6 * LANES), ("field", "shard"), 0, 0, tiled=True)
     arrived = arrived.reshape(6 * LANES, LANES)
-    scale = jnp.asarray(scale_rows())
     update, answers = pl.pallas_call(
         solve_kernel,
         out_shape=(shape((SIZE, LANES), F32), shape((LANES, LANES), F32)),
@@ -582,7 +598,7 @@
         ],
         compiler_params=pltpu.CompilerParams(vmem_limit_bytes=12 << 20),
         name="solve",
-    )(arrived, jnp.asarray(expansion()), scale)
+    )(arrived, expand, scale)
     replies = lax.all_to_all(answers.reshape(LANES, 1, LANES), ("field", "shard"), 0, 0, tiled=True)
     star_update, ccd_update = pl.pallas_call(
         star_kernel,

time: 50.5 us -> 47.3 us (0.937)
  Pallas kernels: 12.1 us -> 8.89 us
    pallas_call x1, Pallas kernels: 5.8 us -> 3.76 us  [shards(): pl.pallas_call(moments_kernel, out_shape=(shape((6 * LANES, LANES), F32),...]
    pallas_call x1, Pallas kernels: 4.77 us -> 3.6 us  [shards(): pl.pallas_call(solve_kernel, out_shape=(shape((SIZE, LANES), F32), shape(...]
where the time goes in v3:
time: 47.3 us; the launch traced here: 47.1 us
  blocking collectives  37.5 us (79%)
  Pallas kernels  8.89 us (19%)
  between operations  0.67 us (1%)
    all_to_all x1, blocking collectives, shards(): lax.all_to_all(outgoing.reshape(LANES, 1, 6 * LANES), ('field', 'shard'),...  23.4 us
    all_to_all x1, blocking collectives, shards(): lax.all_to_all(answers.reshape(LANES, 1, LANES), ('field', 'shard'), 0, 0...  14.1 us
    pallas_call x1, Pallas kernels, shards(): pl.pallas_call(moments_kernel, out_shape=(shape((6 * LANES, LANES), F32),...  3.76 us
    pallas_call x1, Pallas kernels, shards(): pl.pallas_call(solve_kernel, out_shape=(shape((SIZE, LANES), F32), shape(...  3.6 us
    pallas_call x1, Pallas kernels, shards(): pl.pallas_call(star_kernel, out_shape=(shape((tiles, 2, LANES), F32), sha...  1.53 us

profile of v3, /device:TPU:1, one launch (start us, length us, event | category | flops | bytes accessed | tf_op | source)
XLA Modules:
  0.0 47.1 jit_solution(7606436717001994592)
XLA Ops:
  0.6 3.8 %moments.1 = (f32[768,128]{1,0:T(8,128)S(1)}, f32[2,128,128]{2,1,0:T(8,128)S(1)}, s32[8,128]{1,0:T(8,128)S(1)}, bf16[3,896,192]{2,1,0:T(8,128)(2,1)S(1)}, f32[32,128]{1,0:T(8,128)S(1)}) custom-call(f32[192,128]{1,0:T(8,128)} %bitcast.25, f32[192,128]{1,0:T(8,128)} %bitcast.17, f32[192,128]{1,0:T(8,128)} %bitcast.19, f32[6,16,128]{2,1,0:T(8,128)} %bitcast.22, ...), custom_call_target="tpu_custom_call" | custom-call | tf_op jit(solution)/shard_map/moments/pallas_call | solution.py:563
  4.4 0.0 copy-start
  4.4 0.0 copy-start.1
  4.4 0.0 copy-start.2
  4.4 23.4 %all_to_all.10 = f32[128,1,768]{2,1,0:T(1,128)S(1)} all-to-all(f32[128,1,768]{2,1,0:T(1,128)S(1)} %bitcast.16), channel_id=1, replica_groups=mesh['field'=4,'shard'=32] {'field','shard'}, dimensions={0} | all-to-all | bytes 786432 | tf_op jit(solution)/shard_map/all_to_all | solution.py:585
  27.8 3.6 %solve.1 = (f32[56,128]{1,0:T(8,128)}, f32[128,128]{1,0:T(8,128)S(1)}) custom-call(f32[768,128]{1,0:T(8,128)S(1)} %bitcast.15, bf16[3,896,192]{2,1,0:T(8,128)(2,1)S(1)} %get-tuple-element.16.expand_ref, f32[32,128]{1,0:T(8,128)S(1)} %get-tuple-element.14.scale_ref), custom_call_target="tpu_custom_call" | custom-call | tf_op jit(solution)/shard_map/solve/pallas_call | solution.py:587
  31.4 14.1 %all_to_all.11 = f32[128,1,128]{2,1,0:T(1,128)S(1)} all-to-all(f32[128,1,128]{2,1,0:T(1,128)S(1)} %bitcast.24), channel_id=1, replica_groups=mesh['field'=4,'shard'=32] {'field','shard'}, dimensions={0} | all-to-all | bytes 131072 | tf_op jit(solution)/shard_map/all_to_all | solution.py:602
  45.5 0.0 copy-done
  45.5 0.0 copy-done.1
  45.5 0.0 copy-done.2
  45.6 1.5 %stars.1 = (f32[16,2,128]{2,1,0:T(2,128)}, f32[6,189]{1,0:T(8,128)}) custom-call(f32[192,128]{1,0:T(8,128)S(1)} %bitcast.18, f32[192,128]{1,0:T(8,128)S(1)} %bitcast.20, f32[6,16,128]{2,1,0:T(8,128)S(1)} %bitcast.23, f32[2,128,128]{2,1,0:T(8,128)S(1)} %get-tuple-element.12.uvt_ref, s32[8,128]{1,0:T(8,128)S(1)} %get-tuple-element.13.where_ref, ...), custom_call_target="tpu_custom_call" | custom-call | tf_op jit(solution)/shard_map/stars/pallas_call | solution.py:603
Async XLA Ops:
  4.4 41.1 %copy-start = (f32[16,6,2,128]{3,2,1,0:T(2,128)S(1)}, f32[16,6,2,128]{3,2,1,0:T(2,128)}, u32[]{:S(2)}) copy-start(f32[16,6,2,128]{3,2,1,0:T(2,128)} %param.11) | copy-start | bytes 294916
  4.4 41.1 %copy-start.1 = (f32[16,6,2,128]{3,2,1,0:T(2,128)S(1)}, f32[16,6,2,128]{3,2,1,0:T(2,128)}, u32[]{:S(2)}) copy-start(f32[16,6,2,128]{3,2,1,0:T(2,128)} %param.12) | copy-start | bytes 294916
  4.4 41.1 %copy-start.2 = (f32[16,6,128]{2,0,1:T(8,128)S(1)}, f32[16,6,128]{2,0,1:T(8,128)}, u32[]{:S(2)}) copy-start(f32[16,6,128]{2,0,1:T(8,128)} %param.13) | copy-start | bytes 147460

commit v4 on v3

--- a/solution.py
+++ b/solution.py
@@ -56,7 +56,7 @@
         parts.append(part)
         rest = rest - part.astype(np.float64)
     high, middle, low = parts
-    return np.stack([np.concatenate(pair, 1) for pair in ((high, high), (middle, middle), (high, low))])
+    return np.concatenate([high, high, middle, middle, high, low], 1)
 
 
 def scale_rows():
@@ -156,22 +156,22 @@
 
 
 def moments_kernel(*refs):
-    sources, out_refs, buffers, (sems, *scratch) = refs[:10], refs[10:15], refs[15:23], refs[23:]
+    sources, out_refs, buffers, (sems, *scratch) = refs[:10], refs[10:17], refs[17:25], refs[25:]
     copies = [
         pltpu.make_async_copy(source, buffer, sems.at[at])
-        for at, (source, buffer) in enumerate(zip(sources, (*buffers, *out_refs[3:])))
+        for at, (source, buffer) in enumerate(zip(sources, (*buffers, *out_refs[5:])))
     ]
     for copy in copies:
         copy.start()
     for copy in copies[:8]:
         copy.wait()
-    moments_body(*buffers, *out_refs[:3], *scratch)
+    moments_body(*buffers, *out_refs[:5], *scratch)
     for copy in copies[8:]:
         copy.wait()
 
 
 def moments_body(uv_ref, off_ref, diag_ref, corr_ref, count_ref, ids_ref, ccd_ref, slot_ref,
-                 out_ref, uvt_ref, where_ref, chan, pu, pv, acc, mom):
+                 out_ref, power_ref, where_ref, base_ref, gain_ref, chan, high_power, acc, mom):
     tiles = corr_ref.shape[1]
     visits_all = tiles * VISITS
     sub8 = iota((8, LANES), 0)
@@ -191,7 +191,8 @@
     picked = dot(slot_ref[...].astype(F32), (rows128 == ident // LANES).astype(F32), ((0,), (0,)))
     position = jnp.sum(jnp.where(rows128 == ident % LANES, picked, 0.0), axis=0, keepdims=True)
     position = (position + 0.5).astype(jnp.int32)
-    dest = jnp.where(valid, position // LANES, -1)
+    home = position // LANES
+    dest = jnp.where(valid, home % 32 * 4 + home // 32, -1)
     ccd = jnp.where(valid, ccd, -1)
     dest_t = jnp.broadcast_to(dest.astype(F32), (LANES, LANES)).T.astype(jnp.int32)
     same = (dest_t == dest) & (rows128 < lanes128)
@@ -206,6 +207,8 @@
     grad_x = sum(w[0] * r[0] + w[2] * r[1] for w, r in zip(weights, resid))
     grad_y = sum(w[2] * r[0] + w[1] * r[1] for w, r in zip(weights, resid))
     shift_x, shift_y = apply_inverse(inverse, grad_x, grad_y)
+    base_ref[0] = shift_x
+    base_ref[1] = shift_y
     inv_xx, inv_yy, inv_xy = inverse
     channels = [[] for _ in range(7)]
     for visit in range(VISITS):
@@ -216,6 +219,8 @@
         prod_12 = inv_xx * w_xy + inv_xy * w_yy
         prod_21 = inv_xy * w_xx + inv_yy * w_xy
         prod_22 = inv_xy * w_xy + inv_yy * w_yy
+        for at, product in enumerate((prod_11, prod_12, prod_21, prod_22)):
+            gain_ref[at, pl.ds(visit * tiles, tiles), :] = product
         values = (
             uv_ref[pl.ds(2 * visit, tiles, stride=2 * VISITS), :],
             uv_ref[pl.ds(2 * visit + 1, tiles, stride=2 * VISITS), :],
@@ -229,17 +234,22 @@
             channels[at].append(value)
     for at in range(7):
         chan[at] = jnp.concatenate(channels[at] + [pad], axis=0).T
-    uvt_ref[0] = chan[0]
-    uvt_ref[1] = chan[1]
 
     groups = LANES // 8
 
     for g in range(groups):
         at = pl.ds(g * 8, 8)
-        for ref, source in ((pu, 0), (pv, 1)):
+        for source in range(2):
             for degree, value in enumerate(legendre(chan[source, at, :], DEG2 + 1)):
-                if degree:
-                    ref[degree, at, :] = value
+                if degree > ORDER:
+                    high_power[source, degree - ORDER - 1, at, :] = value
+                elif degree:
+                    power_ref[source, degree - 1, at, :] = value
+
+    def power(source, degree, at):
+        if degree > ORDER:
+            return high_power[source, degree - ORDER - 1, at, :]
+        return power_ref[source, degree - 1, at, :]
 
     def sweep(i, top, first, count, row0, width):
         heights = top - i + 1
@@ -248,10 +258,10 @@
             at = pl.ds(g * 8, 8)
             scaled = [chan[first + w, at, :] for w in range(count)]
             if i:
-                factor = pu[i, at, :]
+                factor = power(0, i, at)
                 scaled = [value * factor for value in scaled]
             for j in range(heights):
-                other = pv[j, at, :] if j else None
+                other = power(1, j, at) if j else None
                 for w in range(count):
                     term = scaled[w] * other if j else scaled[w]
                     before = sums[j * count + w]
@@ -283,18 +293,16 @@
     first = split3(mom[0:256])
     third = split3(jnp.concatenate([mom[256:352], zero32], axis=0))
     fourth = split3(jnp.concatenate([zero96, mom[0:8], mom[96:104], mom[192:200], pulls], axis=0))
-    pair = jnp.concatenate(first[:2], axis=1)
+    first = jnp.concatenate(first, axis=1)
+    last = jnp.concatenate([piece for parts in zip(third, fourth) for piece in parts], axis=1)
     for copy in range(2):
         place = ((rows128 == dest) & (copy_at == copy)).astype(jnp.bfloat16)
         place_det = (rows128 + LANES * copy == ccd).astype(jnp.bfloat16)
-        twice = jnp.concatenate([place, place], axis=1)
-        front = dot16(twice, pair, ((1,), (1,))) + dot16(place, first[2], ((1,), (1,)))
+        front = dot16(jnp.concatenate([place] * 3, axis=1), first, ((1,), (1,)))
         out_ref[rows_of(3 * copy), :] = front[:, 0:LANES]
         out_ref[rows_of(3 * copy + 1), :] = front[:, LANES:]
-        both = jnp.concatenate([place, place_det], axis=1)
-        out_ref[rows_of(3 * copy + 2), :] = sum(
-            dot16(both, jnp.concatenate(parts, axis=1), ((1,), (1,))) for parts in zip(third, fourth)
-        )
+        both = jnp.concatenate([place, place_det] * 3, axis=1)
+        out_ref[rows_of(3 * copy + 2), :] = dot16(both, last, ((1,), (1,)))
 
 
 def detector_solve(table):
@@ -356,11 +364,11 @@
     for copy in range(2):
         column = arr_ref[rows_of(3 * copy), :][:, MARK : MARK + 1]
         picks.append((column.astype(jnp.int32) == lanes128 + 1).astype(jnp.bfloat16))
-    pick = jnp.concatenate(picks, axis=0)
+    pick = jnp.concatenate(picks * 3, axis=0)
     for block in range(3):
         both = jnp.concatenate([arr_ref[rows_of(block), :], arr_ref[rows_of(3 + block), :]], axis=0)
-        table[pl.ds(block * LANES, LANES), :] = sum(
-            dot16(value, pick, ((0,), (0,))) for value in split3(both)
+        table[pl.ds(block * LANES, LANES), :] = dot16(
+            jnp.concatenate(split3(both), axis=0), pick, ((0,), (0,))
         )
 
     sums = [jnp.sum(arr_ref[rows_of(3 * copy + 2), :], axis=0, keepdims=True) for copy in range(2)]
@@ -368,14 +376,10 @@
     answer = detector_solve(turned[96:128])
 
     high, middle, low = split3(jnp.concatenate([table[0:96], table[96:192], table[192:288]], axis=1))
-    upper = jnp.concatenate([high, middle], axis=0)
-    lower = jnp.concatenate([low, high], axis=0)
+    parts = jnp.concatenate([high, middle, high, middle, low, high], axis=0)
     chunk = 128
     for at in range(0, POLY * 32, chunk):
-        sides = ((0, upper), (1, upper), (2, lower))
-        wide[pl.ds(at, chunk), :] = sum(
-            dot16(expand_ref[side, pl.ds(at, chunk), :], values, ((1,), (0,))) for side, values in sides
-        )
+        wide[pl.ds(at, chunk), :] = dot16(expand_ref[pl.ds(at, chunk), :], parts, ((1,), (0,)))
 
     def part(which, q, group):
         return wide[q * 32 + group * 8 : q * 32 + group * 8 + 8, which * LANES : (which + 1) * LANES]
@@ -478,12 +482,15 @@
         ],
         axis=1,
     )
-    resp_ref[...] = sum(dot16(left, value, ((1,), (1,))) for value in split3(right))
-
-
-def star_kernel(off_ref, diag_ref, corr_ref, uvt_ref, where_ref, scale_ref, resp_ref,
-                star_ref, det_ref, coeff, model):
-    tiles = corr_ref.shape[1]
+    left = jnp.concatenate([left] * 3, axis=1)
+    resp_ref[...] = dot16(left, jnp.concatenate(split3(right), axis=1), ((1,), (1,)))
+
+
+def star_kernel(base_ref, gain_ref, power_ref, where_ref, scale_ref, update_ref, resp_ref,
+                star_ref, det_ref, update_out, coeff, model, sem):
+    write = pltpu.make_async_copy(update_ref, update_out, sem)
+    write.start()
+    tiles = base_ref.shape[1]
     rows128 = iota((LANES, LANES), 0)
     turned = resp_ref[...].T
     det_ref[:, 0:LANES] = turned[112:118]
@@ -491,10 +498,12 @@
     dest = where_ref[0:1]
     copy_at = where_ref[1:2]
     ccd = where_ref[2:3]
-    picks = [((rows128 == dest) & (copy_at == c)).astype(F32) for c in range(2)]
-    picks += [(rows128 + LANES * c == ccd).astype(F32) for c in range(2)]
-    exposure = dot(turned[0:56], picks[0], ((1,), (0,))) + dot(turned[56:112], picks[1], ((1,), (0,)))
-    detector = dot(turned[112:120], picks[2], ((1,), (0,))) + dot(turned[120:128], picks[3], ((1,), (0,)))
+    picks = [((rows128 == dest) & (copy_at == c)).astype(jnp.bfloat16) for c in range(2)]
+    dets = [(rows128 + LANES * c == ccd).astype(jnp.bfloat16) for c in range(2)]
+    halves = split3(jnp.concatenate([turned[0:56], turned[56:112]], axis=1))
+    exposure = dot16(jnp.concatenate(halves, axis=1), jnp.concatenate(picks * 3, axis=0), ((1,), (0,)))
+    halves = split3(jnp.concatenate([turned[112:120], turned[120:128]], axis=1))
+    detector = dot16(jnp.concatenate(halves, axis=1), jnp.concatenate(dets * 3, axis=0), ((1,), (0,)))
     scale = scale_ref[...]
     coeff[0:28, :] = exposure[0:28] * scale[0:28]
     coeff[32:60, :] = exposure[28:56] * scale[0:28]
@@ -503,10 +512,10 @@
             row = 32 * axis + TERM_INDEX[term]
             coeff[row : row + 1, :] = coeff[row : row + 1, :] + detector[3 * axis + m : 3 * axis + m + 1]
 
-    def evaluate(g, carry):
-        at = pl.ds(pl.multiple_of(g * 8, 8), 8)
-        in_u = legendre(uvt_ref[0, at, :], ORDER + 1)
-        in_v = legendre(uvt_ref[1, at, :], ORDER + 1)
+    for g in range(LANES // 8):
+        at = pl.ds(g * 8, 8)
+        in_u = [None] + [power_ref[0, i, at, :] for i in range(ORDER)]
+        in_v = [None] + [power_ref[1, i, at, :] for i in range(ORDER)]
         for axis in range(2):
             total = None
             for i in range(ORDER + 1):
@@ -521,24 +530,17 @@
                     inner = inner * in_u[i]
                 total = inner if total is None else total + inner
             model[axis, at, :] = total
-        return carry
-
-    lax.fori_loop(0, LANES // 8, evaluate, 0, unroll=2)
     model_x = model[0].T
     model_y = model[1].T
-    weights, resid, inverse = star_terms(off_ref, diag_ref, corr_ref, where_ref[3:4, 0:tiles])
-    grad_x = None
+    out_x = base_ref[0]
+    out_y = base_ref[1]
     for visit in range(VISITS):
-        w_xx, w_yy, w_xy = weights[visit]
-        left_x = resid[visit][0] - model_x[visit * tiles : (visit + 1) * tiles]
-        left_y = resid[visit][1] - model_y[visit * tiles : (visit + 1) * tiles]
-        part_x = w_xx * left_x + w_xy * left_y
-        part_y = w_xy * left_x + w_yy * left_y
-        grad_x = part_x if grad_x is None else grad_x + part_x
-        grad_y = part_y if visit == 0 else grad_y + part_y
-    out_x, out_y = apply_inverse(inverse, grad_x, grad_y)
+        at = slice(visit * tiles, (visit + 1) * tiles)
+        out_x = out_x - (gain_ref[0, at, :] * model_x[at] + gain_ref[1, at, :] * model_y[at])
+        out_y = out_y - (gain_ref[2, at, :] * model_x[at] + gain_ref[3, at, :] * model_y[at])
     star_ref[:, 0, :] = out_x
     star_ref[:, 1, :] = out_y
+    write.wait()
 
 
 def vmem(count):
@@ -560,29 +562,30 @@
     )
     shape = jax.ShapeDtypeStruct
     tables = (jnp.asarray(expansion()), jnp.asarray(scale_rows()))
-    outgoing, turned, where, expand, scale = pl.pallas_call(
+    outgoing, powers, where, base, gain, expand, scale = pl.pallas_call(
         moments_kernel,
         out_shape=(
             shape((6 * LANES, LANES), F32),
-            shape((2, LANES, LANES), F32),
+            shape((2, ORDER, LANES, LANES), F32),
             shape((8, LANES), jnp.int32),
+            shape((2, tiles, LANES), F32),
+            shape((4, tiles * VISITS, LANES), F32),
             *(shape(array.shape, array.dtype) for array in tables),
         ),
         in_specs=[pl.BlockSpec(memory_space=pltpu.HBM)] * 10,
-        out_specs=tuple(vmem(5)),
+        out_specs=tuple(vmem(7)),
         scratch_shapes=[pltpu.VMEM(array.shape, array.dtype) for array in inputs]
         + [
             pltpu.SemaphoreType.DMA((10,)),
             pltpu.VMEM((7, LANES, LANES), F32),
-            pltpu.VMEM((DEG2 + 1, LANES, LANES), F32),
-            pltpu.VMEM((DEG2 + 1, LANES, LANES), F32),
+            pltpu.VMEM((2, ORDER, LANES, LANES), F32),
             pltpu.VMEM((ROW_DET * 8, LANES), F32),
             pltpu.VMEM((ROW_DET, LANES), F32),
         ],
         compiler_params=pltpu.CompilerParams(vmem_limit_bytes=12 << 20),
         name="moments",
     )(*(pltpu.with_memory_space_constraint(array, pltpu.HBM) for array in (*inputs, *tables)))
-    arrived = lax.all_to_all(outgoing.reshape(LANES, 1, 6 * LANES), ("field", "shard"), 0, 0, tiled=True)
+    arrived = lax.all_to_all(outgoing.reshape(LANES, 1, 6 * LANES), ("shard", "field"), 0, 0, tiled=True)
     arrived = arrived.reshape(6 * LANES, LANES)
     update, answers = pl.pallas_call(
         solve_kernel,
@@ -599,16 +602,20 @@
         compiler_params=pltpu.CompilerParams(vmem_limit_bytes=12 << 20),
         name="solve",
     )(arrived, expand, scale)
-    replies = lax.all_to_all(answers.reshape(LANES, 1, LANES), ("field", "shard"), 0, 0, tiled=True)
-    star_update, ccd_update = pl.pallas_call(
+    replies = lax.all_to_all(answers.reshape(LANES, 1, LANES), ("shard", "field"), 0, 0, tiled=True)
+    star_update, ccd_update, update = pl.pallas_call(
         star_kernel,
-        out_shape=(shape((tiles, 2, LANES), F32), shape((6, NCCD), F32)),
+        out_shape=(shape((tiles, 2, LANES), F32), shape((6, NCCD), F32), shape((SIZE, LANES), F32)),
         in_specs=vmem(7),
-        out_specs=tuple(vmem(2)),
-        scratch_shapes=[pltpu.VMEM((64, LANES), F32), pltpu.VMEM((2, LANES, LANES), F32)],
+        out_specs=(*vmem(2), pl.BlockSpec(memory_space=pltpu.HBM)),
+        scratch_shapes=[
+            pltpu.VMEM((64, LANES), F32),
+            pltpu.VMEM((2, LANES, LANES), F32),
+            pltpu.SemaphoreType.DMA,
+        ],
         compiler_params=pltpu.CompilerParams(vmem_limit_bytes=12 << 20),
         name="stars",
-    )(*inputs[1:4], turned, where, scale, replies.reshape(LANES, LANES))
+    )(base, gain, powers, where, scale, update, replies.reshape(LANES, LANES))
     return star_update, update, ccd_update.T
 
 

time: 47.3 us -> 46.6 us (0.985)
  no operation moved by 1% of the time
where the time goes in v4:
time: 46.6 us; the launch traced here: 46.4 us
  blocking collectives  37.3 us (80%)
  Pallas kernels  8.42 us (18%)
  between operations  0.65 us (1%)
    all_to_all x1, blocking collectives, shards(): lax.all_to_all(outgoing.reshape(LANES, 1, 6 * LANES), ('shard', 'field'),...  23.9 us
    all_to_all x1, blocking collectives, shards(): lax.all_to_all(answers.reshape(LANES, 1, LANES), ('shard', 'field'), 0, 0...  13.4 us
    pallas_call x1, Pallas kernels, shards(): pl.pallas_call(moments_kernel, out_shape=(shape((6 * LANES, LANES), F32),...  3.91 us
    pallas_call x1, Pallas kernels, shards(): pl.pallas_call(solve_kernel, out_shape=(shape((SIZE, LANES), F32), shape(...  3.28 us
    pallas_call x1, Pallas kernels, shards(): pl.pallas_call(star_kernel, out_shape=(shape((tiles, 2, LANES), F32), sha...  1.23 us

profile of v4, /device:TPU:1, one launch (start us, length us, event | category | flops | bytes accessed | tf_op | source)
XLA Modules:
  0.0 46.4 jit_solution(3110716479164608405)
XLA Ops:
  0.6 3.9 %moments.1 = (f32[768,128]{1,0:T(8,128)S(1)}, f32[2,6,128,128]{3,2,1,0:T(8,128)S(1)}, s32[8,128]{1,0:T(8,128)S(1)}, f32[2,16,128]{2,1,0:T(8,128)S(1)}, f32[4,96,...) custom-call(f32[192,128]{1,0:T(8,128)} %bitcast.19, f32[192,128]{1,0:T(8,128)} %bitcast.20, ...), custom_call_target="tpu_custom_call" | custom-call | tf_op jit(solution)/shard_map/moments/pallas_call | solution.py:565
  4.5 23.9 %all_to_all.10 = f32[128,1,768]{2,1,0:T(1,128)S(1)} all-to-all(f32[128,1,768]{2,1,0:T(1,128)S(1)} %bitcast.16), channel_id=1, replica_groups=mesh['field'=4,'shard'=32] {'shard','field'}, dimensions={0} | all-to-all | bytes 786432 | tf_op jit(solution)/shard_map/all_to_all | solution.py:588
  28.4 3.3 %solve.1 = (f32[56,128]{1,0:T(8,128)S(1)}, f32[128,128]{1,0:T(8,128)S(1)}) custom-call(f32[768,128]{1,0:T(8,128)S(1)} %bitcast.15, bf16[896,576]{1,0:T(8,128)(2,1)S(1)} %get-tuple-element.21.expand_ref, f32[32,128]{1,0:T(8,128)S(1)} %get-tuple-element.19.scale_ref), custom_call_target="tpu_custom_call" | custom-call | tf_op jit(solution)/shard_map/solve/pallas_call | solution.py:590
  31.7 13.4 %all_to_all.11 = f32[128,1,128]{2,1,0:T(1,128)S(1)} all-to-all(f32[128,1,128]{2,1,0:T(1,128)S(1)} %bitcast.18), channel_id=1, replica_groups=mesh['field'=4,'shard'=32] {'shard','field'}, dimensions={0} | all-to-all | bytes 131072 | tf_op jit(solution)/shard_map/all_to_all | solution.py:605
  45.2 1.2 %stars.1 = (f32[16,2,128]{2,1,0:T(2,128)}, f32[6,189]{1,0:T(8,128)}, f32[56,128]{1,0:T(8,128)}) custom-call(f32[2,16,128]{2,1,0:T(8,128)S(1)} %get-tuple-element.15.base_ref, f32[4,96,128]{2,1,0:T(8,128)S(1)} %get-tuple-element.16.gain_ref, f32[2,6,128,128]{3,2,1,0:T(8,128)S(1)} %get-tuple-element.17.power_ref, s32[8,128]{1,0:T(8,128)S(1)} %get-tuple-element.18.where_ref, ...), custom_call_target="tpu_custom_call" | custom-call | tf_op jit(solution)/shard_map/stars/pallas_call | solution.py:606

commit v5 on v4

--- a/solution.py
+++ b/solution.py
@@ -18,16 +18,18 @@
 DETECTOR_DAMP = 1.0
 HIGH = lax.Precision.HIGHEST
 DEG2 = 2 * ORDER
+UNROLL = 8
 F32 = jnp.float32
 
 TERMS = [(i, n - i) for n in range(DEG2 + 1) for i in range(n + 1)]
 TERM_INDEX = {term: at for at, term in enumerate(TERMS)}
-SCALE = [math.sqrt((2 * i + 1) * (2 * j + 1)) for i, j in TERMS[:POLY]]
-
-ROW_GX = 288
-ROW_GY = 320
+LEAD = [math.factorial(2 * n) / (2**n * math.factorial(n) ** 2) for n in range(DEG2 + 1)]
+NORM = [math.sqrt((2 * i + 1) * (2 * j + 1)) for i, j in TERMS[:POLY]]
+SCALE = [norm * LEAD[i] * LEAD[j] for norm, (i, j) in zip(NORM, TERMS)]
+
+ROW_GX = 96
+ROW_GY = 224
 ROW_DET = 352
-ROWS = 384
 MARK = 95
 
 
@@ -44,11 +46,12 @@
 
 def expansion():
     table = linearisation()
-    matrix = np.zeros((POLY * 32, 96))
+    matrix = np.zeros((POLY * 32, LANES))
     for q, (iq, jq) in enumerate(TERMS[:POLY]):
         for p, (ip, jp) in enumerate(TERMS[:POLY]):
             for at, (a, b) in enumerate(TERMS):
-                matrix[q * 32 + p, at] = SCALE[p] * SCALE[q] * table[ip, iq, a] * table[jp, jq, b]
+                product = table[ip, iq, a] * LEAD[a] * table[jp, jq, b] * LEAD[b]
+                matrix[q * 32 + p, at] = NORM[p] * NORM[q] * product
     parts = []
     rest = matrix
     for _ in range(3):
@@ -56,7 +59,7 @@
         parts.append(part)
         rest = rest - part.astype(np.float64)
     high, middle, low = parts
-    return np.concatenate([high, high, middle, middle, high, low], 1)
+    return np.concatenate([high, middle, low], 1)
 
 
 def scale_rows():
@@ -91,8 +94,8 @@
 def legendre(value, count):
     values = [None, value]
     for degree in range(1, count - 1):
-        lower = (degree / (degree + 1)) * (values[degree - 1] if degree > 1 else 1.0)
-        values.append(((2 * degree + 1) / (degree + 1)) * value * values[degree] - lower)
+        before = values[degree - 1] if degree > 1 else 1.0
+        values.append(value * values[degree] - (degree * degree / (4 * degree * degree - 1)) * before)
     return values
 
 
@@ -140,19 +143,6 @@
                 merged.append(jnp.where(low, a + pltpu.roll(a, 8 - shift, 0), b + pltpu.roll(b, shift, 0)))
         values = merged
     return values[0]
-
-
-def transpose8(values, sub):
-    values = list(values)
-    for shift in (4, 2, 1):
-        low = (sub & shift) == 0
-        for at in range(8):
-            if at & shift:
-                continue
-            a, b = values[at], values[at + shift]
-            values[at] = jnp.where(low, a, pltpu.roll(b, shift, 0))
-            values[at + shift] = jnp.where(low, pltpu.roll(a, 8 - shift, 0), b)
-    return values
 
 
 def moments_kernel(*refs):
@@ -253,35 +243,39 @@
 
     def sweep(i, top, first, count, row0, width):
         heights = top - i + 1
-        sums = [None] * (heights * count)
-        for g in range(groups):
-            at = pl.ds(g * 8, 8)
+
+        def step(g, sums):
+            at = pl.ds(pl.multiple_of(g * 8, 8), 8)
             scaled = [chan[first + w, at, :] for w in range(count)]
             if i:
                 factor = power(0, i, at)
                 scaled = [value * factor for value in scaled]
+            new = []
             for j in range(heights):
                 other = power(1, j, at) if j else None
                 for w in range(count):
                     term = scaled[w] * other if j else scaled[w]
-                    before = sums[j * count + w]
-                    sums[j * count + w] = term if before is None else before + term
+                    new.append(sums[j * count + w] + term)
+            return tuple(new)
+
+        start = tuple(jnp.zeros((8, LANES), F32) for _ in range(heights * count))
+        sums = lax.fori_loop(0, groups, step, start, unroll=UNROLL)
         for j in range(heights):
             for w in range(count):
                 row = row0 + w * width + TERM_INDEX[(i, j)]
                 acc[pl.ds(row * 8, 8), :] = sums[j * count + w]
 
     for i in range(DEG2 + 1):
-        sweep(i, DEG2, 2, 3, 0, 96)
+        sweep(i, DEG2, 2, 3, 0, LANES)
     for i in range(ORDER + 1):
-        sweep(i, ORDER, 5, 2, ROW_GX, 32)
+        sweep(i, ORDER, 5, 2, ROW_GX, LANES)
     zero = jnp.zeros((8, LANES), F32)
     for block in range(3):
         for row in range(len(TERMS), 96):
-            acc[pl.ds((block * 96 + row) * 8, 8), :] = zero
+            acc[pl.ds((block * LANES + row) * 8, 8), :] = zero
     for block in range(2):
         for row in range(POLY, 32):
-            acc[pl.ds((ROW_GX + block * 32 + row) * 8, 8), :] = zero
+            acc[pl.ds((ROW_GX + block * LANES + row) * 8, 8), :] = zero
 
     for g in range(ROW_DET // 8):
         mom[pl.ds(g * 8, 8), :] = combine([acc[pl.ds(g * 64 + 8 * s, 8), :] for s in range(8)], sub8)
@@ -292,7 +286,7 @@
     zero96 = jnp.zeros((96, LANES), F32)
     first = split3(mom[0:256])
     third = split3(jnp.concatenate([mom[256:352], zero32], axis=0))
-    fourth = split3(jnp.concatenate([zero96, mom[0:8], mom[96:104], mom[192:200], pulls], axis=0))
+    fourth = split3(jnp.concatenate([zero96, mom[0:8], mom[128:136], mom[256:264], pulls], axis=0))
     first = jnp.concatenate(first, axis=1)
     last = jnp.concatenate([piece for parts in zip(third, fourth) for piece in parts], axis=1)
     for copy in range(2):
@@ -311,8 +305,8 @@
 
     def block_of(block):
         one, u, v = moment(block, 0, 0), moment(block, 1, 0), moment(block, 0, 1)
-        uu = (2.0 * moment(block, 2, 0) + one) * (1.0 / 3.0)
-        vv = (2.0 * moment(block, 0, 2) + one) * (1.0 / 3.0)
+        uu = moment(block, 2, 0) + one * (1.0 / 3.0)
+        vv = moment(block, 0, 2) + one * (1.0 / 3.0)
         uv = moment(block, 1, 1)
         return [[one, u, v], [u, uu, uv], [v, uv, vv]]
 
@@ -355,53 +349,61 @@
 PANEL = 4
 
 
-def solve_kernel(arr_ref, expand_ref, scale_ref, upd_ref, resp_ref, table, wide, mat, rhs, invs):
+def solve_kernel(arr_ref, expand_ref, scale_ref, upd_ref, resp_ref, wide, mat, rhs, invs, inv_rows):
     sub8 = iota((8, LANES), 0)
     rows128 = iota((LANES, LANES), 0)
     lanes128 = iota((LANES, LANES), 1)
 
-    picks = []
-    for copy in range(2):
-        column = arr_ref[rows_of(3 * copy), :][:, MARK : MARK + 1]
-        picks.append((column.astype(jnp.int32) == lanes128 + 1).astype(jnp.bfloat16))
-    pick = jnp.concatenate(picks * 3, axis=0)
-    for block in range(3):
-        both = jnp.concatenate([arr_ref[rows_of(block), :], arr_ref[rows_of(3 + block), :]], axis=0)
-        table[pl.ds(block * LANES, LANES), :] = dot16(
-            jnp.concatenate(split3(both), axis=0), pick, ((0,), (0,))
-        )
+    marks = [arr_ref[rows_of(3 * copy), :] for copy in range(2)]
+    picks = [(mark[:, MARK : MARK + 1].astype(jnp.int32) == lanes128 + 1).astype(jnp.bfloat16) for mark in marks]
+    pick = [
+        (mark.T[MARK : MARK + 1].astype(jnp.int32) == rows128 + 1).astype(jnp.bfloat16) for mark in marks
+    ]
+    slots = [
+        jnp.concatenate([marks[copy]] + [arr_ref[rows_of(3 * copy + block), :] for block in (1, 2)], axis=1)
+        for copy in range(2)
+    ]
+    slots = split3(jnp.concatenate(slots, axis=0))
+    table = dot16(jnp.concatenate(pick * 3, axis=1), jnp.concatenate(slots, axis=0), ((1,), (0,)))
 
     sums = [jnp.sum(arr_ref[rows_of(3 * copy + 2), :], axis=0, keepdims=True) for copy in range(2)]
     turned = jnp.where(rows128 == 0, sums[0], jnp.where(rows128 == 1, sums[1], 0.0)).T
     answer = detector_solve(turned[96:128])
 
-    high, middle, low = split3(jnp.concatenate([table[0:96], table[96:192], table[192:288]], axis=1))
-    parts = jnp.concatenate([high, middle, high, middle, low, high], axis=0)
-    chunk = 128
-    for at in range(0, POLY * 32, chunk):
-        wide[pl.ds(at, chunk), :] = dot16(expand_ref[pl.ds(at, chunk), :], parts, ((1,), (0,)))
+    pieces = []
+    for block in range(3):
+        high, middle, low = split3(table[:, block * LANES : (block + 1) * LANES])
+        pieces.append(jnp.concatenate([high, middle, high, middle, low, high], axis=1))
+    parts = jnp.concatenate(pieces, axis=0)
+
+    def expand(q0):
+        at = pl.ds(q0 * 32, PANEL * 32)
+        left = [expand_ref[at, side * LANES : (side + 1) * LANES] for side in (0, 0, 1, 1, 0, 2)]
+        wide[at, :] = dot16(jnp.concatenate(left, axis=1), parts, ((1,), (1,)))
 
     def part(which, q, group):
         return wide[q * 32 + group * 8 : q * 32 + group * 8 + 8, which * LANES : (which + 1) * LANES]
 
-    for col, (kind, q) in enumerate(UNKNOWNS):
-        for group in range(col // 8, BLOCKS):
-            if kind == "x":
-                if group < 3:
-                    value = part(0, q, group)
-                elif group == 3:
-                    value = jnp.where(sub8 < 4, part(0, q, 3), pltpu.roll(part(2, q, 3), 4, 0))
-                else:
-                    value = part(2, q, group - 4)
+    def entry(col, group):
+        kind, q = UNKNOWNS[col]
+        if kind == "x":
+            if group < 3:
+                value = part(0, q, group)
             elif group == 3:
-                value = jnp.where(sub8 < 4, 0.0, pltpu.roll(part(1, q, 3), 4, 0))
+                value = jnp.where(sub8 < 4, part(0, q, 3), pltpu.roll(part(2, q, 3), 4, 0))
             else:
-                value = part(1, q, group - 4)
-            if group == col // 8:
-                value = value + jnp.where(sub8 == col % 8, EXPOSURE_DAMP, 0.0)
-            mat[pl.ds(col * SIZE + group * 8, 8), :] = value
-    grad_x = table[ROW_GX : ROW_GX + 32] * scale_ref[...]
-    grad_y = table[ROW_GY : ROW_GY + 32] * scale_ref[...]
+                value = part(2, q, group - 4)
+        elif group == 3:
+            value = jnp.where(sub8 < 4, 0.0, pltpu.roll(part(1, q, 3), 4, 0))
+        else:
+            value = part(1, q, group - 4)
+        if group == col // 8:
+            value = value + jnp.where(sub8 == col % 8, EXPOSURE_DAMP, 0.0)
+        return value
+
+    expand(0)
+    grad_x = table[:, 0:LANES].T[96:128] * scale_ref[...]
+    grad_y = table[:, LANES : 2 * LANES].T[96:128] * scale_ref[...]
     rhs[0:24, :] = grad_x[0:24]
     rhs[24:32, :] = jnp.where(sub8 < 4, grad_x[24:32], pltpu.roll(grad_y[24:32], 4, 0))
     rhs[32:56, :] = grad_y[0:24]
@@ -420,9 +422,9 @@
                     new.append(carry[c * count + g] - column[g] * factor)
             return tuple(new)
 
-        panel = tuple(
-            mat[pl.ds((k0 + c) * SIZE + g * 8, 8), :] for c in range(PANEL) for g in range(g0, BLOCKS)
-        )
+        if k0 + PANEL < POLY:
+            expand(k0 + PANEL)
+        panel = tuple(entry(k0 + c, g) for c in range(PANEL) for g in range(g0, BLOCKS))
         for j in range(k0):
             panel = update(j, panel)
         panel = [list(panel[c * count : (c + 1) * count]) for c in range(PANEL)]
@@ -442,6 +444,16 @@
             invs[k : k + 1, :] = inverse
             for g in range(count):
                 mat[pl.ds(k * SIZE + (g0 + g) * 8, 8), :] = column[g]
+        if (k0 + PANEL) % 8 == 0:
+            inverted = []
+            for row in range(8):
+                value = jnp.where(sub8 == row, 1.0, 0.0)
+                for before in range(row):
+                    factor = mat[pl.ds((g0 * 8 + before) * SIZE + g0 * 8 + row, 1), :]
+                    value = value - factor * inverted[before]
+                value = value * invs[pl.ds(g0 * 8 + row, 1), :]
+                inverted.append(value)
+                inv_rows[pl.ds((g0 * 8 + row) * 8, 8), :] = value
         for g in range(count):
             rhs[pl.ds((g0 + g) * 8, 8), :] = right[g]
 
@@ -457,11 +469,10 @@
                     total = term if total is None else total + term
                 partial.append(total)
             right = right - combine(partial, sub8)
-        diagonal = transpose8([mat[pl.ds((b * 8 + c) * SIZE + b * 8, 8), :] for c in range(8)], sub8)
-        for c in range(7, -1, -1):
-            value = right[c : c + 1] * invs[b * 8 + c : b * 8 + c + 1]
-            right = jnp.where(sub8 < c, right - diagonal[c] * value, jnp.where(sub8 == c, value, right))
-        solved[b] = right
+        terms = [inv_rows[pl.ds((b * 8 + c) * 8, 8), :] * right[c : c + 1] for c in range(8)]
+        while len(terms) > 1:
+            terms = [terms[at] + terms[at + 1] for at in range(0, len(terms), 2)]
+        solved[b] = terms[0]
     whole = jnp.concatenate(
         solved[0:3] + [solved[3][0:4]] + solved[4:7] + [solved[3][4:8]], axis=0
     )
@@ -593,11 +604,11 @@
         in_specs=vmem(3),
         out_specs=tuple(vmem(2)),
         scratch_shapes=[
-            pltpu.VMEM((ROWS, LANES), F32),
             pltpu.VMEM((POLY * 32, 3 * LANES), F32),
             pltpu.VMEM((SIZE * SIZE, LANES), F32),
             pltpu.VMEM((SIZE, LANES), F32),
             pltpu.VMEM((SIZE, LANES), F32),
+            pltpu.VMEM((SIZE * 8, LANES), F32),
         ],
         compiler_params=pltpu.CompilerParams(vmem_limit_bytes=12 << 20),
         name="solve",

time: 46.6 us -> 46.6 us (level)
  no operation moved by 1% of the time
where the time goes in v5:
time: 46.6 us; the launch traced here: 46.4 us
  blocking collectives  37.3 us (80%)
  Pallas kernels  8.41 us (18%)
  between operations  0.65 us (1%)
    all_to_all x1, blocking collectives, shards(): lax.all_to_all(outgoing.reshape(LANES, 1, 6 * LANES), ('shard', 'field'),...  23.9 us
    all_to_all x1, blocking collectives, shards(): lax.all_to_all(answers.reshape(LANES, 1, LANES), ('shard', 'field'), 0, 0...  13.4 us
    pallas_call x1, Pallas kernels, shards(): pl.pallas_call(moments_kernel, out_shape=(shape((6 * LANES, LANES), F32),...  3.92 us
    pallas_call x1, Pallas kernels, shards(): pl.pallas_call(solve_kernel, out_shape=(shape((SIZE, LANES), F32), shape(...  3.26 us
    pallas_call x1, Pallas kernels, shards(): pl.pallas_call(star_kernel, out_shape=(shape((tiles, 2, LANES), F32), sha...  1.23 us

profile of v5, /device:TPU:1, one launch (start us, length us, event | category | flops | bytes accessed | tf_op | source)
XLA Modules:
  0.0 46.4 jit_solution(9071961261719904530)
XLA Ops:
  0.6 3.9 %moments.1 = (f32[768,128]{1,0:T(8,128)S(1)}, f32[2,6,128,128]{3,2,1,0:T(8,128)S(1)}, s32[8,128]{1,0:T(8,128)S(1)}, f32[2,16,128]{2,1,0:T(8,128)S(1)}, f32[4,96,...) custom-call(f32[192,128]{1,0:T(8,128)} %bitcast.19, f32[192,128]{1,0:T(8,128)} %bitcast.20, ...), custom_call_target="tpu_custom_call" | custom-call | tf_op jit(solution)/shard_map/moments/pallas_call | solution.py:576
  4.6 23.9 %all_to_all.10 = f32[128,1,768]{2,1,0:T(1,128)S(1)} all-to-all(f32[128,1,768]{2,1,0:T(1,128)S(1)} %bitcast.16), channel_id=1, replica_groups=mesh['field'=4,'shard'=32] {'shard','field'}, dimensions={0} | all-to-all | bytes 786432 | tf_op jit(solution)/shard_map/all_to_all | solution.py:599
  28.5 3.3 %solve.1 = (f32[56,128]{1,0:T(8,128)S(1)}, f32[128,128]{1,0:T(8,128)S(1)}) custom-call(f32[768,128]{1,0:T(8,128)S(1)} %bitcast.15, bf16[896,384]{1,0:T(8,128)(2,1)S(1)} %get-tuple-element.21.expand_ref, f32[32,128]{1,0:T(8,128)S(1)} %get-tuple-element.19.scale_ref), custom_call_target="tpu_custom_call" | custom-call | tf_op jit(solution)/shard_map/solve/pallas_call | solution.py:601
  31.7 13.4 %all_to_all.11 = f32[128,1,128]{2,1,0:T(1,128)S(1)} all-to-all(f32[128,1,128]{2,1,0:T(1,128)S(1)} %bitcast.18), channel_id=1, replica_groups=mesh['field'=4,'shard'=32] {'shard','field'}, dimensions={0} | all-to-all | bytes 131072 | tf_op jit(solution)/shard_map/all_to_all | solution.py:616
  45.2 1.2 %stars.1 = (f32[16,2,128]{2,1,0:T(2,128)}, f32[6,189]{1,0:T(8,128)}, f32[56,128]{1,0:T(8,128)}) custom-call(f32[2,16,128]{2,1,0:T(8,128)S(1)} %get-tuple-element.15.base_ref, f32[4,96,128]{2,1,0:T(8,128)S(1)} %get-tuple-element.16.gain_ref, f32[2,6,128,128]{3,2,1,0:T(8,128)S(1)} %get-tuple-element.17.power_ref, s32[8,128]{1,0:T(8,128)S(1)} %get-tuple-element.18.where_ref, ...), custom_call_target="tpu_custom_call" | custom-call | tf_op jit(solution)/shard_map/stars/pallas_call | solution.py:617

commit v6 on v5

--- a/solution.py
+++ b/solution.py
@@ -16,7 +16,6 @@
 STAR_DAMP = 0.1
 EXPOSURE_DAMP = 1.0
 DETECTOR_DAMP = 1.0
-HIGH = lax.Precision.HIGHEST
 DEG2 = 2 * ORDER
 UNROLL = 8
 F32 = jnp.float32
@@ -68,10 +67,6 @@
     return rows
 
 
-def dot(a, b, dims):
-    return lax.dot_general(a, b, (dims, ((), ())), precision=HIGH, preferred_element_type=F32)
-
-
 def split3(value):
     high = value.astype(jnp.bfloat16)
     rest = value - high.astype(F32)
@@ -178,16 +173,22 @@
     rows128 = iota((LANES, LANES), 0)
     lanes128 = iota((LANES, LANES), 1)
     valid = iota((1, LANES), 1) < visits_all
-    picked = dot(slot_ref[...].astype(F32), (rows128 == ident // LANES).astype(F32), ((0,), (0,)))
-    position = jnp.sum(jnp.where(rows128 == ident % LANES, picked, 0.0), axis=0, keepdims=True)
-    position = (position + 0.5).astype(jnp.int32)
-    home = position // LANES
+    slot = slot_ref[...]
+    digits = jnp.concatenate([slot // LANES, slot % LANES], axis=1).astype(F32).astype(jnp.bfloat16)
+    picked = dot16(digits, (rows128 == ident // LANES).astype(jnp.bfloat16), ((0,), (0,)))
+    inside = rows128 == ident % LANES
+
+    def digit(at):
+        chosen = jnp.where(inside, picked[at * LANES : (at + 1) * LANES], 0.0)
+        return (jnp.sum(chosen, axis=0, keepdims=True) + 0.5).astype(jnp.int32)
+
+    home, place_in = digit(0), digit(1)
     dest = jnp.where(valid, home % 32 * 4 + home // 32, -1)
     ccd = jnp.where(valid, ccd, -1)
     dest_t = jnp.broadcast_to(dest.astype(F32), (LANES, LANES)).T.astype(jnp.int32)
     same = (dest_t == dest) & (rows128 < lanes128)
     copy_at = jnp.sum(same.astype(F32), axis=0, keepdims=True).astype(jnp.int32)
-    mark = (position % LANES + 1).astype(F32)
+    mark = (place_in + 1).astype(F32)
     counts = jnp.concatenate([count_ref[...]] * (LANES // tiles), axis=1)
     where_ref[...] = jnp.where(
         sub8 == 0, dest, jnp.where(sub8 == 1, copy_at, jnp.where(sub8 == 2, ccd, counts))
@@ -402,6 +403,7 @@
         return value
 
     expand(0)
+    expand(PANEL)
     grad_x = table[:, 0:LANES].T[96:128] * scale_ref[...]
     grad_y = table[:, LANES : 2 * LANES].T[96:128] * scale_ref[...]
     rhs[0:24, :] = grad_x[0:24]
@@ -422,8 +424,8 @@
                     new.append(carry[c * count + g] - column[g] * factor)
             return tuple(new)
 
-        if k0 + PANEL < POLY:
-            expand(k0 + PANEL)
+        if k0 + 2 * PANEL < POLY:
+            expand(k0 + 2 * PANEL)
         panel = tuple(entry(k0 + c, g) for c in range(PANEL) for g in range(g0, BLOCKS))
         for j in range(k0):
             panel = update(j, panel)

time: 46.6 us -> 46.5 us (level)
  no operation moved by 1% of the time
where the time goes in v6:
time: 46.5 us; the launch traced here: 46.4 us
  blocking collectives  37.3 us (80%)
  Pallas kernels  8.37 us (18%)
  between operations  0.65 us (1%)
    all_to_all x1, blocking collectives, shards(): lax.all_to_all(outgoing.reshape(LANES, 1, 6 * LANES), ('shard', 'field'),...  23.9 us
    all_to_all x1, blocking collectives, shards(): lax.all_to_all(answers.reshape(LANES, 1, LANES), ('shard', 'field'), 0, 0...  13.4 us
    pallas_call x1, Pallas kernels, shards(): pl.pallas_call(moments_kernel, out_shape=(shape((6 * LANES, LANES), F32),...  3.88 us
    pallas_call x1, Pallas kernels, shards(): pl.pallas_call(solve_kernel, out_shape=(shape((SIZE, LANES), F32), shape(...  3.26 us
    pallas_call x1, Pallas kernels, shards(): pl.pallas_call(star_kernel, out_shape=(shape((tiles, 2, LANES), F32), sha...  1.23 us

profile of v6, /device:TPU:1, one launch (start us, length us, event | category | flops | bytes accessed | tf_op | source)
XLA Modules:
  0.0 46.4 jit_solution(13720919806819195262)
XLA Ops:
  0.6 3.9 %moments.1 = (f32[768,128]{1,0:T(8,128)S(1)}, f32[2,6,128,128]{3,2,1,0:T(8,128)S(1)}, s32[8,128]{1,0:T(8,128)S(1)}, f32[2,16,128]{2,1,0:T(8,128)S(1)}, f32[4,96,...) custom-call(f32[192,128]{1,0:T(8,128)} %bitcast.19, f32[192,128]{1,0:T(8,128)} %bitcast.20, ...), custom_call_target="tpu_custom_call" | custom-call | tf_op jit(solution)/shard_map/moments/pallas_call | solution.py:578
  4.5 23.9 %all_to_all.10 = f32[128,1,768]{2,1,0:T(1,128)S(1)} all-to-all(f32[128,1,768]{2,1,0:T(1,128)S(1)} %bitcast.16), channel_id=1, replica_groups=mesh['field'=4,'shard'=32] {'shard','field'}, dimensions={0} | all-to-all | bytes 786432 | tf_op jit(solution)/shard_map/all_to_all | solution.py:601
  28.4 3.3 %solve.1 = (f32[56,128]{1,0:T(8,128)S(1)}, f32[128,128]{1,0:T(8,128)S(1)}) custom-call(f32[768,128]{1,0:T(8,128)S(1)} %bitcast.15, bf16[896,384]{1,0:T(8,128)(2,1)S(1)} %get-tuple-element.21.expand_ref, f32[32,128]{1,0:T(8,128)S(1)} %get-tuple-element.19.scale_ref), custom_call_target="tpu_custom_call" | custom-call | tf_op jit(solution)/shard_map/solve/pallas_call | solution.py:603
  31.7 13.4 %all_to_all.11 = f32[128,1,128]{2,1,0:T(1,128)S(1)} all-to-all(f32[128,1,128]{2,1,0:T(1,128)S(1)} %bitcast.18), channel_id=1, replica_groups=mesh['field'=4,'shard'=32] {'shard','field'}, dimensions={0} | all-to-all | bytes 131072 | tf_op jit(solution)/shard_map/all_to_all | solution.py:618
  45.1 1.2 %stars.1 = (f32[16,2,128]{2,1,0:T(2,128)}, f32[6,189]{1,0:T(8,128)}, f32[56,128]{1,0:T(8,128)}) custom-call(f32[2,16,128]{2,1,0:T(8,128)S(1)} %get-tuple-element.15.base_ref, f32[4,96,128]{2,1,0:T(8,128)S(1)} %get-tuple-element.16.gain_ref, f32[2,6,128,128]{3,2,1,0:T(8,128)S(1)} %get-tuple-element.17.power_ref, s32[8,128]{1,0:T(8,128)S(1)} %get-tuple-element.18.where_ref, ...), custom_call_target="tpu_custom_call" | custom-call | tf_op jit(solution)/shard_map/stars/pallas_call | solution.py:619

commit v7 on v6

--- a/solution.py
+++ b/solution.py
@@ -17,7 +17,7 @@
 EXPOSURE_DAMP = 1.0
 DETECTOR_DAMP = 1.0
 DEG2 = 2 * ORDER
-UNROLL = 8
+UNROLL = 4
 F32 = jnp.float32
 
 TERMS = [(i, n - i) for n in range(DEG2 + 1) for i in range(n + 1)]

time: 46.5 us -> 46.8 us (level)
  no operation moved by 1% of the time
where the time goes in v7:
time: 46.8 us; the launch traced here: 46.6 us
  blocking collectives  37.3 us (80%)
  Pallas kernels  8.65 us (18%)
  between operations  0.65 us (1%)
    all_to_all x1, blocking collectives, shards(): lax.all_to_all(outgoing.reshape(LANES, 1, 6 * LANES), ('shard', 'field'),...  23.9 us
    all_to_all x1, blocking collectives, shards(): lax.all_to_all(answers.reshape(LANES, 1, LANES), ('shard', 'field'), 0, 0...  13.4 us
    pallas_call x1, Pallas kernels, shards(): pl.pallas_call(moments_kernel, out_shape=(shape((6 * LANES, LANES), F32),...  4.16 us
    pallas_call x1, Pallas kernels, shards(): pl.pallas_call(solve_kernel, out_shape=(shape((SIZE, LANES), F32), shape(...  3.26 us
    pallas_call x1, Pallas kernels, shards(): pl.pallas_call(star_kernel, out_shape=(shape((tiles, 2, LANES), F32), sha...  1.23 us

profile of v7, /device:TPU:1, one launch (start us, length us, event | category | flops | bytes accessed | tf_op | source)
XLA Modules:
  0.0 46.6 jit_solution(7986001913880705395)
XLA Ops:
  0.6 4.2 %moments.1 = (f32[768,128]{1,0:T(8,128)S(1)}, f32[2,6,128,128]{3,2,1,0:T(8,128)S(1)}, s32[8,128]{1,0:T(8,128)S(1)}, f32[2,16,128]{2,1,0:T(8,128)S(1)}, f32[4,96,...) custom-call(f32[192,128]{1,0:T(8,128)} %bitcast.19, f32[192,128]{1,0:T(8,128)} %bitcast.20, ...), custom_call_target="tpu_custom_call" | custom-call | tf_op jit(solution)/shard_map/moments/pallas_call | solution.py:578
  4.8 23.9 %all_to_all.10 = f32[128,1,768]{2,1,0:T(1,128)S(1)} all-to-all(f32[128,1,768]{2,1,0:T(1,128)S(1)} %bitcast.16), channel_id=1, replica_groups=mesh['field'=4,'shard'=32] {'shard','field'}, dimensions={0} | all-to-all | bytes 786432 | tf_op jit(solution)/shard_map/all_to_all | solution.py:601
  28.7 3.3 %solve.1 = (f32[56,128]{1,0:T(8,128)S(1)}, f32[128,128]{1,0:T(8,128)S(1)}) custom-call(f32[768,128]{1,0:T(8,128)S(1)} %bitcast.15, bf16[896,384]{1,0:T(8,128)(2,1)S(1)} %get-tuple-element.21.expand_ref, f32[32,128]{1,0:T(8,128)S(1)} %get-tuple-element.19.scale_ref), custom_call_target="tpu_custom_call" | custom-call | tf_op jit(solution)/shard_map/solve/pallas_call | solution.py:603
  32.0 13.4 %all_to_all.11 = f32[128,1,128]{2,1,0:T(1,128)S(1)} all-to-all(f32[128,1,128]{2,1,0:T(1,128)S(1)} %bitcast.18), channel_id=1, replica_groups=mesh['field'=4,'shard'=32] {'shard','field'}, dimensions={0} | all-to-all | bytes 131072 | tf_op jit(solution)/shard_map/all_to_all | solution.py:618
  45.4 1.2 %stars.1 = (f32[16,2,128]{2,1,0:T(2,128)}, f32[6,189]{1,0:T(8,128)}, f32[56,128]{1,0:T(8,128)}) custom-call(f32[2,16,128]{2,1,0:T(8,128)S(1)} %get-tuple-element.15.base_ref, f32[4,96,128]{2,1,0:T(8,128)S(1)} %get-tuple-element.16.gain_ref, f32[2,6,128,128]{3,2,1,0:T(8,128)S(1)} %get-tuple-element.17.power_ref, s32[8,128]{1,0:T(8,128)S(1)} %get-tuple-element.18.where_ref, ...), custom_call_target="tpu_custom_call" | custom-call | tf_op jit(solution)/shard_map/stars/pallas_call | solution.py:619
